TPU v7x, 128 devices: a whole 4x4x4 slice. The times are simulated.
128 devices in a mesh: feat: 4 (over y), label: 32 (over z, x, core).
Axes of the slice: x: 4, y: 4, z: 4, core: 2. Of those that a mesh axis runs over, the one named last changes fastest.
Arguments:
- documents: bfloat16 [160, 1024], P(None, 'label'), may hold values from -6 to 6
- expand_weight: bfloat16 [1024, 32768], P('label', 'feat'), may hold values from -0.1875 to 0.1875
- sparse_weight: bfloat16 [3072, 16, 128, 128], P(('feat', 'label')), may hold values from -0.125 to 0.125
- feature_lists: int32 [3072, 16], replicated, may hold values from 0 to 255, as said below
- positives: int32 [160, 8], replicated, may hold values from 0 to 393215
Outputs:
- grad_expand: bfloat16 [1024, 32768], P('label', 'feat')
- grad_sparse: bfloat16 [3072, 16, 128, 128], P(('feat', 'label'))
Inputs may be any that keep to these rules, and one draw needn't show every extreme that they name: `feature_lists`: within each aligned group of 24 label blocks (taken in order), the entries name exactly 24 distinct feature blocks from each range of 64 consecutive blocks, each named exactly 4 times in the group; the 16 entries of one label block are distinct.
All inputs are finite; a program needn't handle non-finite values.
Results may differ from a plain program's by a relative error of at most 0.014.
Values may be sent and summed in bfloat16 or wider, within the bound.
A program may use at most 192 MiB of HBM per device.

v0:
```python
import jax
import jax.numpy as jnp
from jax import lax
from jax.sharding import Mesh
from jax.sharding import PartitionSpec as P

BLK = 128
FBLOCKS = 256
SLOTS = 16
LBLK_DEV = 24
CAP = 24
LABEL = ("label_0", "label_1", "label_2")
FEAT_LABEL = ("feat", "label_0", "label_1", "label_2")


def cut_along(x, dim, count):
    before, after = (x.shape[:dim], x.shape[dim + 1 :])
    return jnp.moveaxis(x.reshape(*before, count, -1, *after), dim, 0)


def joined_along(pieces, dim):
    pieces = jnp.moveaxis(pieces, 0, dim)
    shape = pieces.shape
    return pieces.reshape(*shape[:dim], shape[dim] * shape[dim + 1], *shape[dim + 2 :])


def exchange_in_order(pieces, axes, sequence):
    inside = pieces.shape[1:]
    whole = pieces.reshape(*(lax.axis_size(a) for a in axes), *inside)
    for k in sequence:
        whole = lax.all_to_all(whole, axes[k], k, k, tiled=True)
    return whole.reshape(-1, *inside)


def core_and_chips(x, groups, sequence, split_dim, concat_dim):
    count = lax.axis_size(groups[0]) * lax.axis_size(groups[1])
    pieces = cut_along(x, split_dim, count)
    return joined_along(exchange_in_order(pieces, groups, sequence), concat_dim)


def from_everyone(x, axis):
    copies = jnp.broadcast_to(x, (lax.axis_size(axis), *x.shape))
    return lax.all_to_all(copies, axis, split_axis=0, concat_axis=0, tiled=True)


def collect(x, axis, dim):
    pieces = from_everyone(x, axis)
    return joined_along(pieces, dim)


def on_device(documents, expand_weight, sparse_weight, feature_lists, positives):
    feat_count = lax.axis_size("feat")
    label_count = lax.axis_size(LABEL)
    feat_index = lax.axis_index("feat")
    label_index = lax.axis_index(LABEL)
    group = feat_index * label_count + label_index
    doc_count = documents.shape[0]
    own_count = expand_weight.shape[1] // BLK
    column_weight = core_and_chips(expand_weight, (("label_0", "label_1"), "label_2"), (1, 0), 1, 0)
    docs_full = collect(documents, LABEL, 1)
    hidden_cols = jnp.maximum(
        jnp.dot(docs_full, column_weight, preferred_element_type=jnp.float32), 0.0
    ).astype(jnp.bfloat16)
    hidden_flat = collect(hidden_cols, LABEL, 1)
    hidden = hidden_flat.reshape(doc_count, own_count, BLK).transpose(1, 0, 2)
    mine = lax.dynamic_slice_in_dim(feature_lists, group * LBLK_DEV, LBLK_DEV, 0)

    def sender_list(target):
        rows = lax.dynamic_slice_in_dim(
            feature_lists, (target * label_count + label_index) * LBLK_DEV, LBLK_DEV, 0
        )
        local_ids = feat_index * own_count + jnp.arange(own_count, dtype=jnp.int32)
        used = jnp.any(rows.reshape(-1)[:, None] == local_ids[None, :], axis=0)
        order = jnp.argsort(jnp.where(used, 0, 1).astype(jnp.int32), stable=True)
        return order[:CAP]

    send_index = jax.vmap(sender_list)(jnp.arange(feat_count, dtype=jnp.int32))
    outgoing = jnp.take(hidden, send_index, axis=0)
    incoming = lax.all_to_all(outgoing, "feat", split_axis=0, concat_axis=0, tiled=True)
    present = jnp.any(
        mine.reshape(-1)[:, None] == jnp.arange(FBLOCKS, dtype=jnp.int32)[None, :], axis=0
    )
    ranks = jnp.cumsum(present.reshape(feat_count, own_count).astype(jnp.int32), axis=1) - 1
    position_table = (jnp.arange(feat_count, dtype=jnp.int32)[:, None] * CAP + ranks).reshape(-1)
    slot_position = jnp.take(position_table, mine, axis=0)
    picked = jnp.take(incoming.reshape(feat_count * CAP, doc_count, BLK), slot_position, axis=0)
    logits = jnp.einsum("lsdc,lsce->dle", picked, sparse_weight, preferred_element_type=jnp.float32)
    label_ids = (group * LBLK_DEV + jnp.arange(LBLK_DEV, dtype=jnp.int32))[
        :, None
    ] * BLK + jnp.arange(BLK, dtype=jnp.int32)[None, :]
    targets = jnp.any(positives[:, :, None, None] == label_ids[None, None, :, :], axis=1).astype(
        jnp.float32
    )
    residual = (jax.nn.sigmoid(logits) - targets).astype(jnp.bfloat16)
    grad_sparse = jnp.einsum(
        "lsdc,dle->lsce", picked, residual, preferred_element_type=jnp.float32
    ).astype(jnp.bfloat16)
    back = jnp.einsum("dle,lsce->lsdc", residual, sparse_weight, preferred_element_type=jnp.float32)
    back_rows = back.reshape(LBLK_DEV * SLOTS, doc_count, BLK)
    group_part = jax.ops.segment_sum(
        back_rows, slot_position.reshape(-1), num_segments=feat_count * CAP
    )
    group_part = group_part.astype(jnp.bfloat16).reshape(feat_count, CAP, doc_count, BLK)
    returned = lax.all_to_all(group_part, "feat", split_axis=0, concat_axis=0, tiled=True)
    column_sum = jax.ops.segment_sum(
        returned.astype(jnp.float32).reshape(feat_count * CAP, doc_count, BLK),
        send_index.reshape(-1),
        num_segments=own_count,
    )
    flat_grad = column_sum.transpose(1, 0, 2).reshape(doc_count, own_count * BLK)
    share_cols = lax.psum_scatter(
        flat_grad.astype(jnp.bfloat16), LABEL, scatter_dimension=1, tiled=True
    ).astype(jnp.float32)
    hidden_grad_cols = jnp.where(hidden_cols > 0, share_cols, 0.0).astype(jnp.bfloat16)
    grad_cols = jnp.dot(docs_full.T, hidden_grad_cols, preferred_element_type=jnp.float32).astype(
        jnp.bfloat16
    )
    grad_expand = core_and_chips(grad_cols, (("label_0", "label_1"), "label_2"), (1, 0), 0, 1)
    return (grad_expand, grad_sparse)


def solution(mesh):
    finer = Mesh(
        mesh.devices.reshape(mesh.shape["feat"], 4, 4, 2), ("feat", "label_0", "label_1", "label_2")
    )
    return jax.shard_map(
        on_device,
        mesh=finer,
        in_specs=(P(None, LABEL), P(LABEL, "feat"), P(FEAT_LABEL, None, None, None), P(), P()),
        out_specs=(P(LABEL, "feat"), P(FEAT_LABEL, None, None, None)),
        check_vma=False,
    )
```

profile of v0, /device:TPU:1, one launch (start us, length us, event | category | flops | bytes accessed | tf_op | source)
XLA Modules:
  0.0 497.1 jit_solution(10945641511947916780)
XLA Ops:
  8.7 5.2 %all_to_all.40 = bf16[16,2,32,256]{3,2,0,1:T(8,128)(2,1)S(1)} all-to-all(bf16[16,2,32,256]{3,2,0,1:T(8,128)(2,1)S(1)} %copy.65), channel_id=1, replica_groups=mesh['feat'=4,'label_0'=4,'label_1'=4,'label_2'=2] {'label_2'}, dimensions={1} | all-to-all | bytes 1048576 | tf_op jit(solution)/shard_map/all_to_all | solution.py:31
  15.4 8.4 %all-to-all-start = ((bf16[32,160,32]{1,2,0:T(8,128)(2,1)}), bf16[32,160,32]{1,2,0:T(8,128)(2,1)S(1)}, u32[]{:S(2)}, u32[]{:S(2)}) async-start(bf16[32,160,32]{1,2,0:T(8,128)(2,1)} %broadcast_in_dim.64), calls=%async_computation | async-start | bytes 1048576 | tf_op jit(solution)/shard_map/all_to_all | solution.py:43
  23.9 11.5 %all-to-all-done = bf16[32,160,32]{1,2,0:T(8,128)(2,1)S(1)} async-done(((bf16[32,160,32]{1,2,0:T(8,128)(2,1)}), bf16[32,160,32]{1,2,0:T(8,128)(2,1)S(1)}, u32[]{:S(2)}, u32[]{:S(2)}) %all-to-all-start) | async-done | bytes 327712 | tf_op jit(solution)/shard_map/all_to_all | solution.py:43
  35.4 13.9 %all_to_all.41 = bf16[16,2,32,256]{3,2,1,0:T(8,128)(2,1)S(1)} all-to-all(bf16[16,2,32,256]{3,2,1,0:T(8,128)(2,1)S(1)} %copy.66), channel_id=1, replica_groups=mesh['feat'=4,'label_0'=4,'label_1'=4,'label_2'=2] {'label_0','label_1'}, dimensions={0} | all-to-all | bytes 1048576 | tf_op jit(solution)/shard_map/all_to_all | solution.py:31
  51.4 5.4 %all-to-all-start.3 = ((bf16[32,160,256]{2,1,0:T(8,128)(2,1)}), bf16[32,160,256]{2,1,0:T(8,128)(2,1)S(1)}, u32[]{:S(2)}, u32[]{:S(2)}) async-start(bf16[32,160,256]{2,1,0:T(8,128)(2,1)} %broadcast_in_dim.74), calls=%async_computation.3 | async-start | bytes 5242880 | tf_op jit(solution)/shard_map/all_to_all | solution.py:43
  56.8 8.6 %while.1 = (s32[]{:T(128)}, s32[3072,16]{0,1:T(8,128)}, s32[4,2]{0,1:T(2,128)S(1)}, s32[4,24,16]{1,2,0:T(8,128)S(1)}, s32[]{:T(128)}) while((s32[]{:T(128)}, s32[3072,16]{0,1:T(8,128)}, s32[4,2]{0,1:T(2,128)S(1)}, s32[4,24,16]{1,2,0:T(8,128)S(1)}, s32[]{:T(128)}) %tuple.22), condition=%wide.while_cond, body=%wide.while_body.sunk | while | flops 2 | bytes 9825 | solution.py:69
  67.3 23.1 %all-to-all-done.3 = bf16[32,160,256]{2,1,0:T(8,128)(2,1)S(1)} async-done(((bf16[32,160,256]{2,1,0:T(8,128)(2,1)}), bf16[32,160,256]{2,1,0:T(8,128)(2,1)S(1)}, u32[]{:S(2)}, u32[]{:S(2)}) %all-to-all-start.3) | async-done | bytes 2621472 | tf_op jit(solution)/shard_map/all_to_all | solution.py:43
  93.4 5.0 %reshape_reshape.10 = bf16[160,64,128]{2,1,0:T(8,128)(2,1)} reshape(bf16[160,32,256]{2,1,0:T(8,128)(2,1)} %copy.72) | data formatting | bytes 5242880 | tf_op jit(solution)/shard_map/reshape;reshape | solution.py:65
  104.9 4.5 broadcast_select_fusion.5
  109.4 5.0 %all-to-all-start.4 = ((bf16[4,24,160,128]{3,2,1,0:T(8,128)(2,1)}), bf16[4,24,160,128]{3,2,1,0:T(8,128)(2,1)}, u32[]{:S(2)}, u32[]{:S(2)}) async-start(bf16[4,24,160,128]{3,2,1,0:T(8,128)(2,1)} %broadcast_select_fusion.5), calls=%async_computation.4 | async-start | bytes 7864320 | tf_op jit(solution)/shard_map/all_to_all | solution.py:79
  123.1 34.7 %all-to-all-done.4 = bf16[4,24,160,128]{3,2,1,0:T(8,128)(2,1)} async-done(((bf16[4,24,160,128]{3,2,1,0:T(8,128)(2,1)}), bf16[4,24,160,128]{3,2,1,0:T(8,128)(2,1)}, u32[]{:S(2)}, u32[]{:S(2)}) %all-to-all-start.4) | async-done | bytes 3932192 | tf_op jit(solution)/shard_map/all_to_all | solution.py:79
  157.8 14.8 %gather_fusion.2 = bf16[384,160,128]{2,1,0:T(8,128)(2,1)} fusion(bf16[96,160,128]{2,1,0:T(8,128)(2,1)} %bitcast.8, s32[1024]{0:T(1024)S(1)} %pad_clamp_fusion), kind=kCustom, calls=%fused_computation.2 | custom fusion | bytes 31458816 | tf_op jit(solution)/shard_map/jit(_take)/gather | solution.py:86
  172.6 11.4 %fusion.9 = bf16[160,24,128,1]{2,0,3,1:T(8,128)(2,1)S(1)} fusion(pred[160,24,128]{2,1,0:T(8,128)(4,1)S(1)} %compare_reduce_fusion, bf16[24,16,128,128]{3,2,1,0:T(8,128)(2,1)} %param.7, bf16[24,16,160,128]{3,2,1,0:T(8,128)(2,1)} %bitcast.76, pred[24,16]{1,0:T(8,128)(4,1)S(1)} %get-tuple-element.20), kind=kOutput, calls=%fused_computation.25 | convolution fusion | flops 2024079360 | bytes 29786496 | tf_op jit(solution)/shard_map/lsdc,lsce->dle/dot_general | solution.py:87
  184.0 15.2 %fusion.19 = f32[24,160,16,128]{3,1,2,0:T(8,128)} fusion(bf16[160,24,128,1]{2,0,3,1:T(8,128)(2,1)S(1)} %fusion.9, bf16[24,16,128,128]{3,2,1,0:T(8,128)(2,1)} %param.7), kind=kOutput, calls=%fused_computation.57 | convolution fusion | flops 2013265920 | bytes 45023232 | tf_op jit(solution)/shard_map/dle,lsce->lsdc/dot_general | solution.py:98
  203.4 87.4 %scatter_fusion = f32[96,160,128]{2,1,0:T(8,128)} fusion(f32[96,160,128]{2,1,0:T(8,128)} %broadcast_in_dim.69, s32[384]{0:T(512)S(1)} %reshape.202, f32[384,160,128]{2,1,0:T(8,128)} %bitcast.74), kind=kCustom, calls=%fused_computation.3 | custom fusion | flops 7864320 | bytes 94373376 | tf_op jit(solution)/shard_map/scatter-add | solution.py:100
  290.8 5.8 %convert_element_type.48 = bf16[96,160,128]{2,1,0:T(8,128)(2,1)} convert(f32[96,160,128]{2,1,0:T(8,128)} %scatter_fusion) | non-fusion elementwise | flops 1966080 | bytes 11796480 | tf_op jit(solution)/shard_map/convert_element_type | solution.py:103
  296.7 4.8 all-to-all-start.5
  301.9 42.1 %all-to-all-done.5 = bf16[4,24,160,128]{3,2,1,0:T(8,128)(2,1)} async-done(((bf16[4,24,160,128]{3,2,1,0:T(8,128)(2,1)}), bf16[4,24,160,128]{3,2,1,0:T(8,128)(2,1)}, u32[]{:S(2)}, u32[]{:S(2)}) %all-to-all-start.5) | async-done | bytes 3932192 | tf_op jit(solution)/shard_map/all_to_all | solution.py:104
  344.0 6.4 %bitcast_convert_fusion = f32[96,160,128]{2,1,0:T(8,128)} fusion(bf16[4,24,160,128]{3,2,1,0:T(8,128)(2,1)} %all-to-all-done.5), kind=kLoop, calls=%fused_computation.14 | loop fusion | flops 1966080 | bytes 11796480 | tf_op jit(solution)/shard_map/reshape | solution.py:106
  353.4 22.6 %scatter_fusion.1 = f32[64,160,128]{2,1,0:T(8,128)} fusion(f32[64,160,128]{2,1,0:T(8,128)} %broadcast_in_dim.65, s32[96]{0:T(128)S(1)} %reshape.210, f32[96,160,128]{2,1,0:T(8,128)} %bitcast_convert_fusion), kind=kCustom, calls=%fused_computation.4 | custom fusion | flops 1966080 | bytes 23593344 | tf_op jit(solution)/shard_map/scatter-add | solution.py:105
  380.4 81.8 %reduce-scatter.2.cloned.1.call-done = bf16[160,256]{1,0:T(8,128)(2,1)} async-done(((bf16[160,8192]{1,0:T(8,128)(2,1)}), bf16[160,256]{1,0:T(8,128)(2,1)}) %reduce-scatter.2.cloned.1.call-update) | async-done | bytes 81936 | tf_op jit(solution)/shard_map/reduce_scatter | solution.py:111
  463.7 6.1 %all_to_all.42 = bf16[16,2,32,256]{3,2,0,1:T(8,128)(2,1)S(1)} all-to-all(bf16[16,2,32,256]{3,2,0,1:T(8,128)(2,1)S(1)} %copy.79), channel_id=1, replica_groups=mesh['feat'=4,'label_0'=4,'label_1'=4,'label_2'=2] {'label_2'}, dimensions={1} | all-to-all | bytes 1048576 | tf_op jit(solution)/shard_map/all_to_all | solution.py:31
  470.6 4.7 all-to-all-start.7
  475.3 14.1 %fusion.4 = bf16[24,16,128,128]{3,2,1,0:T(8,128)(2,1)} fusion(bf16[160,24,128,1]{2,0,3,1:T(8,128)(2,1)S(1)} %fusion.9, bf16[24,16,160,128]{3,2,1,0:T(8,128)(2,1)} %bitcast.77, pred[24,16]{1,0:T(8,128)(4,1)S(1)} %get-tuple-element.20), kind=kOutput, calls=%fused_computation.13 | convolution fusion | flops 2027421696 | bytes 29294976 | tf_op jit(solution)/shard_map/lsdc,dle->lsce/dot_general | solution.py:95
  (78 shorter events, 48.9 us)
Async XLA Ops:
  15.4 19.9 %all-to-all-start = ((bf16[32,160,32]{1,2,0:T(8,128)(2,1)}), bf16[32,160,32]{1,2,0:T(8,128)(2,1)S(1)}, u32[]{:S(2)}, u32[]{:S(2)}) async-start(bf16[32,160,32]{1,2,0:T(8,128)(2,1)} %broadcast_in_dim.64), calls=%async_computation | async-start | bytes 1048576 | tf_op jit(solution)/shard_map/all_to_all | solution.py:43
  51.4 39.0 %all-to-all-start.3 = ((bf16[32,160,256]{2,1,0:T(8,128)(2,1)}), bf16[32,160,256]{2,1,0:T(8,128)(2,1)S(1)}, u32[]{:S(2)}, u32[]{:S(2)}) async-start(bf16[32,160,256]{2,1,0:T(8,128)(2,1)} %broadcast_in_dim.74), calls=%async_computation.3 | async-start | bytes 5242880 | tf_op jit(solution)/shard_map/all_to_all | solution.py:43
  109.4 48.4 %all-to-all-start.4 = ((bf16[4,24,160,128]{3,2,1,0:T(8,128)(2,1)}), bf16[4,24,160,128]{3,2,1,0:T(8,128)(2,1)}, u32[]{:S(2)}, u32[]{:S(2)}) async-start(bf16[4,24,160,128]{3,2,1,0:T(8,128)(2,1)} %broadcast_select_fusion.5), calls=%async_computation.4 | async-start | bytes 7864320 | tf_op jit(solution)/shard_map/all_to_all | solution.py:79
  114.4 4.8 copy-start
  296.7 47.3 %all-to-all-start.5 = ((bf16[4,24,160,128]{3,2,1,0:T(8,128)(2,1)}), bf16[4,24,160,128]{3,2,1,0:T(8,128)(2,1)}, u32[]{:S(2)}, u32[]{:S(2)}) async-start(bf16[4,24,160,128]{3,2,1,0:T(8,128)(2,1)} %bitcast.78), calls=%async_computation.5 | async-start | bytes 7864320 | tf_op jit(solution)/shard_map/all_to_all | solution.py:104
  301.5 160.7 %reduce-scatter.2.cloned.1.call-start = ((), (), s32[]{:S(2)}) async-start(), calls=%async_computation.9 | async-start | bytes 2703360 | tf_op jit(solution)/shard_map/reduce_scatter | solution.py:111
  470.6 18.8 %all-to-all-start.7 = ((bf16[16,2,32,256]{3,2,1,0:T(8,128)(2,1)}), bf16[16,2,32,256]{3,2,1,0:T(8,128)(2,1)S(1)}, u32[]{:S(2)}, u32[]{:S(2)}) async-start(bf16[16,2,32,256]{3,2,1,0:T(8,128)(2,1)} %copy.80), calls=%async_computation.8 | async-start | bytes 1048576 | tf_op jit(solution)/shard_map/all_to_all | solution.py:31
Sparse Core Ops, SparseCore 0:
  380.5 81.6 reduce-scatter.1
where the time goes:
time: 500 us; the launch traced here: 497 us
  waiting for transfers between devices  193 us (39%)
  other arithmetic  137 us (27%)
  local copies, waits for them, and re-layouts  56.9 us (11%)
  matrix products  42.3 us (8%)
  starting transfers between devices  28.5 us (6%)
  blocking collectives  25.2 us (5%)
  between operations  14.3 us (3%)
    scatter-add x1, other arithmetic, on_device(): jax.ops.segment_sum(back_rows, slot_position.reshape(-1), num_segments=fe...  87.4 us
    reduce_scatter x1, waiting for transfers between devices, on_device(): lax.psum_scatter(flat_grad.astype(jnp.bfloat16), LABEL, scatter_dimension...  81.8 us
    all_to_all x1, waiting for transfers between devices, on_device(): lax.all_to_all(group_part, 'feat', split_axis=0, concat_axis=0, tiled=True)  42.1 us
    all_to_all x1, waiting for transfers between devices, on_device(): lax.all_to_all(outgoing, 'feat', split_axis=0, concat_axis=0, tiled=True)  34.7 us
    all_to_all x2, waiting for transfers between devices, from_everyone(): return lax.all_to_all(copies, axis, split_axis=0, concat_axis=0, tiled=True)  34.6 us
    all_to_all x3, blocking collectives, exchange_in_order(): whole = lax.all_to_all(whole, axes[k], k, k, tiled=True)  25.2 us
    scatter-add x1, other arithmetic, on_device(): jax.ops.segment_sum(returned.astype(jnp.float32).reshape(feat_count * CAP...  22.6 us
    dot_general x1, matrix products, on_device(): jnp.einsum('dle,lsce->lsdc', residual, sparse_weight, preferred_element_t...  15.2 us
  transfers between devices with their start and end apart: 6, of which 5 were waited for; matrix products, arithmetic and copies ran while one was open for 7% of the time, Pallas kernels for 0%

commit v1 on v0

v1 whole, which is shorter than its diff:
```python
import functools

import jax
import jax.numpy as jnp
from jax import lax
from jax.experimental import pallas as pl
from jax.experimental.pallas import tpu as pltpu
from jax.sharding import Mesh
from jax.sharding import PartitionSpec as P

BLK = 128
FBLOCKS = 256
SLOTS = 16
LBLK_DEV = 24
POOL = 96
NAMED = 4
POS = 8
DOCS = 160
HALF = 80
SHARD = 320
RING = 4
AXES = ("feat", "label_0", "label_1", "label_2")
LABEL = AXES[1:]
MESH = pl.DeviceIdType.MESH
MIB = 1 << 20

PARTS = (((2, 0, 1), 0, 112), ((0, 1, 2), 112, 112), ((1, 2, 0), 224, 96))
PLANE_PARTS = (((0, 1), 0, 160), ((1, 0), 160, 160))


def hop(m, k):
    return lax.rem(m + k, RING)


def region(part, phase, here, t, half, lead=()):
    order, row, rows = part
    index = list(here)
    cut = rows // 32 * 16
    span = {None: (row, rows), 0: (row, rows - cut), 1: (row + rows - cut, cut)}
    low, size = span[half] if phase == 0 else (row, rows)
    for done in range(phase):
        index[order[done]] = slice(None)
    if phase > 0 and half is not None:
        index[order[phase - 1]] = pl.ds(2 * half, 2)
    index[order[phase]] = t
    return (*index, *lead, pl.ds(low, size), slice(None))


def ring_gather(buf, parts, here, axes, lead, send, recv, first_source, on_phase, on_chunk):
    def copy(p, phase, way, k, source_t, half, source=None):
        axis = parts[p][0][phase]
        at = region(parts[p], phase, here, source_t, half, lead)
        slot = ((p * len(axes) + phase) * 2 + way) * 3 + k
        src = buf.at[at] if source is None else source(p, half)
        return pltpu.make_async_remote_copy(
            src_ref=src,
            dst_ref=buf.at[at],
            send_sem=send.at[slot],
            recv_sem=recv.at[slot],
            device_id={axes[axis]: hop(here[axis], (1, 3)[way])},
            device_id_type=MESH,
        )

    for phase in range(len(axes)):
        source = first_source if phase == 0 else None
        started = []
        for k in range(2):
            for p in range(len(parts)):
                m = here[parts[p][0][phase]]
                for way in range(2):
                    op = copy(p, phase, way, k, m, k if way == 0 else 1 - k, source)
                    op.start()
                    started.append(op)
        on_phase(phase)
        for p in range(len(parts)):
            m = here[parts[p][0][phase]]
            for way in range(2):
                near = hop(m, (3, 1)[way])
                copy(p, phase, way, 0, near, way).wait_recv()
                op = copy(p, phase, way, 2, near, way)
                op.start()
                started.append(op)
        for p in range(len(parts)):
            m = here[parts[p][0][phase]]
            for way in range(2):
                near = hop(m, (3, 1)[way])
                copy(p, phase, way, 1, near, 1 - way).wait_recv()
                on_chunk(p, phase, near)
        for p in range(len(parts)):
            m = here[parts[p][0][phase]]
            for way in range(2):
                copy(p, phase, way, 2, hop(m, 2), way).wait_recv()
            on_chunk(p, phase, hop(m, 2))
        for op in started:
            op.wait_send()


def expand_kernel(
    docs_ref, weight_ref, hid_ref, docs_all, w_all, shard,
    w_send, w_recv, d_send, d_recv, own_sem, send, recv, sib_send, sib_recv,
):
    y, z, x, c = (lax.axis_index(a) for a in AXES)
    me = z * 8 + x * 2 + c
    sibling = {"label_2": 1 - c}

    def peer(l):
        return {
            "label_0": lax.div(l, 8),
            "label_1": lax.rem(lax.div(l, 2), 4),
            "label_2": lax.rem(l, 2),
        }

    barrier = pltpu.get_barrier_semaphore()

    def greet(o, carry):
        pl.semaphore_signal(
            barrier, inc=1, device_id=peer(lax.rem(me + o, 32)), device_id_type=MESH
        )
        return carry

    lax.fori_loop(1, 32, greet, 0)
    for k in (1, 3):
        pl.semaphore_signal(barrier, inc=1, device_id={"feat": hop(y, k)}, device_id_type=MESH)
    pl.semaphore_wait(barrier, 33)

    def rows_of(ref, l):
        return ref.at[pl.ds(pl.multiple_of(l * 32, 32), 32), :]

    def columns_for(l):
        return weight_ref.at[:, pl.ds(pl.multiple_of(l * 256, 256), 256)]

    def docs_copy(to, origin):
        return pltpu.make_async_remote_copy(
            src_ref=docs_ref, dst_ref=rows_of(docs_all, origin),
            send_sem=d_send.at[to], recv_sem=d_recv.at[origin],
            device_id=peer(to), device_id_type=MESH,
        )

    def weight_copy(to, origin):
        return pltpu.make_async_remote_copy(
            src_ref=columns_for(to), dst_ref=rows_of(w_all, origin),
            send_sem=w_send.at[to], recv_sem=w_recv.at[origin],
            device_id=peer(to), device_id_type=MESH,
        )

    def start(o, carry):
        to = lax.rem(me + o, 32)
        weight_copy(to, me).start()
        docs_copy(to, me).start()
        return carry

    lax.fori_loop(1, 32, start, 0)
    own_docs = pltpu.make_async_copy(docs_ref, rows_of(docs_all, me), own_sem.at[0])
    own_weight = pltpu.make_async_copy(columns_for(me), rows_of(w_all, me), own_sem.at[1])
    own_docs.start()
    own_weight.start()
    own_docs.wait()
    own_weight.wait()

    def finish(o, carry):
        other = lax.rem(me + o, 32)
        weight_copy(other, other).wait_recv()
        docs_copy(other, other).wait_recv()
        return carry

    lax.fori_loop(1, 32, finish, 0)
    product = lax.dot_general(
        docs_all[...], w_all[...], (((0,), (0,)), ((), ())), preferred_element_type=jnp.float32
    )
    hidden = jnp.maximum(product, 0.0).astype(jnp.bfloat16)
    shard[0:DOCS, :] = hidden[:DOCS, :BLK]
    shard[DOCS:SHARD, :] = hidden[:DOCS, BLK:]
    own_hidden = pltpu.make_async_copy(shard, hid_ref.at[y, z, x, c], own_sem.at[2])
    own_hidden.start()

    def first_source(p, half):
        return shard.at[region(PARTS[p], 0, (y, z, x), 0, half)[-2:]]

    siblings = []

    def to_sibling(p, k, t):
        at = region(PARTS[p], 2, (y, z, x), t, None, (c,))
        op = pltpu.make_async_remote_copy(
            src_ref=hid_ref.at[at], dst_ref=hid_ref.at[at],
            send_sem=sib_send.at[p * 4 + k], recv_sem=sib_recv.at[p * 4 + k],
            device_id=sibling, device_id_type=MESH,
        )
        op.start()
        siblings.append(op)

    def on_phase(phase):
        if phase == 0:
            own_hidden.wait()
        if phase == 2:
            for p in range(3):
                to_sibling(p, 0, (y, z, x)[PARTS[p][0][2]])

    count = [1, 1, 1]

    def on_chunk(p, phase, t):
        if phase == 2:
            to_sibling(p, count[p], t)
            count[p] += 1

    ring_gather(
        hid_ref, PARTS, (y, z, x), AXES[:3], (c,), send, recv, first_source, on_phase, on_chunk
    )
    for op in siblings:
        op.wait_send()
    for p in range(3):
        m = (y, z, x)[PARTS[p][0][2]]
        for k, t in enumerate((m, hop(m, 3), hop(m, 1), hop(m, 2))):
            at = region(PARTS[p], 2, (y, z, x), t, None, (1 - c,))
            pltpu.make_async_remote_copy(
                src_ref=hid_ref.at[at], dst_ref=hid_ref.at[at],
                send_sem=sib_send.at[p * 4 + k], recv_sem=sib_recv.at[p * 4 + k],
                device_id=sibling, device_id_type=MESH,
            ).wait_recv()

    def drain(o, carry):
        to = lax.rem(me + o, 32)
        weight_copy(to, me).wait_send()
        docs_copy(to, me).wait_send()
        return carry

    lax.fori_loop(1, 32, drain, 0)


def expand(docs_t, expand_weight):
    return pl.pallas_call(
        expand_kernel,
        out_shape=jax.ShapeDtypeStruct((4, 4, 4, 2, SHARD, BLK), jnp.bfloat16),
        in_specs=[pl.BlockSpec(memory_space=pltpu.VMEM), pl.BlockSpec(memory_space=pl.ANY)],
        out_specs=pl.BlockSpec(memory_space=pl.ANY),
        scratch_shapes=[
            pltpu.VMEM((1024, 256), jnp.bfloat16),
            pltpu.VMEM((1024, 256), jnp.bfloat16),
            pltpu.VMEM((SHARD, BLK), jnp.bfloat16),
            pltpu.SemaphoreType.DMA((32,)),
            pltpu.SemaphoreType.DMA((32,)),
            pltpu.SemaphoreType.DMA((32,)),
            pltpu.SemaphoreType.DMA((32,)),
            pltpu.SemaphoreType.DMA((3,)),
            pltpu.SemaphoreType.DMA((54,)),
            pltpu.SemaphoreType.DMA((54,)),
            pltpu.SemaphoreType.DMA((12,)),
            pltpu.SemaphoreType.DMA((12,)),
        ],
        compiler_params=pltpu.CompilerParams(
            collective_id=0, has_side_effects=True, vmem_limit_bytes=16 * MIB
        ),
        name="expand",
    )(docs_t, expand_weight)


def label_kernel(
    lists, blocks, named, base, pos_ref, hid_ref, weight_ref, gs_ref, gp_ref,
    h, h_t, w, res, pos_b, gp, place, h_sem, w_sem, gp_sem,
):
    g = pl.program_id(0)

    def block_copy(p):
        b = blocks[p]
        return pltpu.make_async_copy(hid_ref.at[b], h.at[p], h_sem.at[p])

    def weight_copy(q):
        return pltpu.make_async_copy(weight_ref.at[q], w.at[q], w_sem.at[q])

    @pl.when(g == 0)
    def _():
        def begin(p, carry):
            block_copy(p).start()
            place[blocks[p]] = p
            return carry

        lax.fori_loop(0, POOL, begin, 0)

        def begin_weight(q, carry):
            weight_copy(q).start()
            return carry

        lax.fori_loop(0, LBLK_DEV, begin_weight, 0)
        for k in range(POS):
            pos_b[k] = jnp.broadcast_to(pos_ref[:, k : k + 1], (DOCS, BLK))

        def arrive(p, carry):
            block_copy(p).wait()
            h_t[p] = h[p].T
            return carry

        lax.fori_loop(0, POOL, arrive, 0)

    weight_copy(g).wait()
    where = [place[lists[g * SLOTS + s]] for s in range(SLOTS)]
    logits = jnp.zeros((DOCS, BLK), jnp.float32)
    for s in range(0, SLOTS, 2):
        left = jnp.concatenate([h[where[s]], h[where[s + 1]]], axis=1)
        right = w[g, s : s + 2].reshape(2 * BLK, BLK)
        logits += jnp.dot(left, right, preferred_element_type=jnp.float32)
    ids = (base[0] + g) * BLK + lax.broadcasted_iota(jnp.int32, (DOCS, BLK), 1)
    hit = pos_b[0] == ids
    for k in range(1, POS):
        hit = jnp.logical_or(hit, pos_b[k] == ids)
    residual = (jax.nn.sigmoid(logits) - jnp.where(hit, 1.0, 0.0)).astype(jnp.bfloat16)
    res[g] = residual
    for s in range(SLOTS):
        gs_ref[0, s] = jnp.dot(
            h_t[where[s]], residual, preferred_element_type=jnp.float32
        ).astype(jnp.bfloat16)

    def gp_copy(f):
        return pltpu.make_async_copy(
            gp.at[pl.ds(f * 24, 24)], gp_ref.at[pl.ds(f * 24, 24)], gp_sem.at[f]
        )

    @pl.when(g == LBLK_DEV - 1)
    def _():
        for f in range(4):

            def collect(p, carry):
                slots = [named[p * NAMED + k] for k in range(NAMED)]
                pairs = [(lax.div(i, SLOTS), lax.rem(i, SLOTS)) for i in slots]
                left = jnp.concatenate([res[q] for q, _ in pairs], axis=1)
                right = jnp.concatenate([w[q, s] for q, s in pairs], axis=1)
                gp[p] = lax.dot_general(
                    left, right, (((1,), (1,)), ((), ())), preferred_element_type=jnp.float32
                ).astype(jnp.bfloat16)
                return carry

            lax.fori_loop(f * 24, f * 24 + 24, collect, 0)
            gp_copy(f).start()
        for f in range(4):
            gp_copy(f).wait()


def label_blocks(lists, blocks, named, base, positives, hid, sparse_weight):
    return pl.pallas_call(
        label_kernel,
        out_shape=(
            jax.ShapeDtypeStruct((LBLK_DEV, SLOTS, BLK, BLK), jnp.bfloat16),
            jax.ShapeDtypeStruct((POOL, DOCS, BLK), jnp.bfloat16),
        ),
        grid_spec=pltpu.PrefetchScalarGridSpec(
            num_scalar_prefetch=4,
            grid=(LBLK_DEV,),
            in_specs=[
                pl.BlockSpec((DOCS, POS), lambda g, *_: (0, 0)),
                pl.BlockSpec(memory_space=pl.ANY),
                pl.BlockSpec(memory_space=pl.ANY),
            ],
            out_specs=(
                pl.BlockSpec((1, SLOTS, BLK, BLK), lambda g, *_: (g, 0, 0, 0)),
                pl.BlockSpec(memory_space=pl.ANY),
            ),
            scratch_shapes=[
                pltpu.VMEM((POOL, DOCS, BLK), jnp.bfloat16),
                pltpu.VMEM((POOL, BLK, DOCS), jnp.bfloat16),
                pltpu.VMEM((LBLK_DEV, SLOTS, BLK, BLK), jnp.bfloat16),
                pltpu.VMEM((LBLK_DEV, DOCS, BLK), jnp.bfloat16),
                pltpu.VMEM((POS, DOCS, BLK), jnp.int32),
                pltpu.VMEM((POOL, DOCS, BLK), jnp.bfloat16),
                pltpu.SMEM((FBLOCKS,), jnp.int32),
                pltpu.SemaphoreType.DMA((POOL,)),
                pltpu.SemaphoreType.DMA((LBLK_DEV,)),
                pltpu.SemaphoreType.DMA((4,)),
            ],
        ),
        compiler_params=pltpu.CompilerParams(
            dimension_semantics=("arbitrary",), vmem_limit_bytes=48 * MIB
        ),
        name="label_blocks",
    )(lists, blocks, named, base, positives, hid, sparse_weight)


def reduce_kernel(
    table, gp_ref, hid_ref, docs_ref, out_ref,
    own, sib, acc, mask, full, *rest,
):
    bufs, (pair_sem, mask_sem, send, recv, g_send, g_recv, sib_send, sib_recv) = rest[:36], rest[36:]
    y, z, x, c = (lax.axis_index(a) for a in AXES)
    here = (y, z, x)
    sibling = {"label_2": 1 - c}
    barrier = pltpu.get_barrier_semaphore()
    for axis, m in zip(AXES, here):
        for k in (1, 3):
            pl.semaphore_signal(barrier, inc=1, device_id={axis: hop(m, k)}, device_id_type=MESH)
    pl.semaphore_signal(barrier, inc=1, device_id=sibling, device_id_type=MESH)
    pl.semaphore_wait(barrier, 7)

    def docs_half(k):
        return gp_ref.at[:, pl.ds(pl.multiple_of(k * HALF, 16), HALF), :]

    to_pair = pltpu.make_async_remote_copy(
        src_ref=docs_half(1 - c), dst_ref=sib.at[pl.ds(0, POOL)],
        send_sem=pair_sem.at[0], recv_sem=pair_sem.at[1],
        device_id=sibling, device_id_type=MESH,
    )
    to_pair.start()
    mine = pltpu.make_async_copy(docs_half(c), own.at[pl.ds(0, POOL)], pair_sem.at[2])
    mine.start()
    masks = []
    for blk in range(4):
        op = pltpu.make_async_copy(
            hid_ref.at[y, z, x, blk // 2, pl.ds(pl.multiple_of(blk % 2 * DOCS + c * HALF, 16), HALF), :],
            mask.at[pl.ds(blk * HALF, HALF), :],
            mask_sem.at[blk],
        )
        op.start()
        masks.append(op)
    own[POOL] = jnp.zeros((HALF, BLK), jnp.bfloat16)
    sib[POOL] = jnp.zeros((HALF, BLK), jnp.bfloat16)
    mine.wait()
    to_pair.wait()
    for op in masks:
        op.wait()

    def spread(q, carry):
        at = (lax.div(q, 16), lax.rem(lax.div(q, 4), 4), lax.rem(q, 4))
        for blk in range(4):
            b = q * 4 + blk
            acc[(*at, pl.ds(blk * HALF, HALF), slice(None))] = (
                own[table[b]] + sib[table[FBLOCKS + b]]
            )
        return carry

    lax.fori_loop(0, 64, spread, 0)

    def buf(p, phase, kind):
        return bufs[(p * 3 + phase) * 4 + kind]

    def inner(p, phase, half):
        at = region(PARTS[p], phase, here, 0, half)
        order, row, rows = PARTS[p]
        kept = [at[a] for a in range(3) if a in order[:phase]]
        cut = rows // 32 * 16
        span = (0, rows)
        if phase == 0 and half is not None:
            span = ((0, rows - cut), (rows - cut, cut))[half]
        return (*kept, pl.ds(*span), slice(None))

    def push(p, phase, way, k):
        axis = PARTS[p][0][phase]
        m = here[axis]
        near = hop(m, (1, 3)[way])
        t, half = ((hop(m, 2), way), (near, 1 - way), (near, way))[k]
        dst = buf(p, phase, way) if k == 0 else buf(p, phase, 2 + way).at[inner(p, phase, half)]
        slot = ((p * 3 + phase) * 2 + way) * 3 + k
        return pltpu.make_async_remote_copy(
            src_ref=acc.at[region(PARTS[p], phase, here, t, half)], dst_ref=dst,
            send_sem=send.at[slot], recv_sem=recv.at[slot],
            device_id={AXES[axis]: near}, device_id_type=MESH,
        )

    def tiles(p, phase, half, body):
        at = region(PARTS[p], phase, here, 0, half)
        order = PARTS[p][0]
        dims = [a for a in range(3) if a in order[:phase]]
        starts, sizes = [], []
        for a in dims:
            cut = at[a] if not isinstance(at[a], slice) else pl.ds(0, 4)
            starts.append(cut.start)
            sizes.append(cut.size)
        total = 1
        for size in sizes:
            total *= size

        def one(i, carry):
            local = []
            rest_i = i
            for size in reversed(sizes):
                local.insert(0, lax.rem(rest_i, size))
                rest_i = lax.div(rest_i, size)
            body(dims, starts, local)
            return carry

        if total == 1:
            body(dims, starts, [])
        else:
            lax.fori_loop(0, total, one, 0)

    def add_into(p, phase, t, half, sources):
        at = region(PARTS[p], phase, here, t, half)

        def body(dims, starts, local):
            index = list(at)
            for a, first, i in zip(dims, starts, local):
                index[a] = first + i
            total = acc[tuple(index)].astype(jnp.float32)
            for source, whole in sources:
                lead = [first + i for first, i in zip(starts, local)] if whole else local
                total = total + source[(*lead, slice(None), slice(None))].astype(jnp.float32)
            acc[tuple(index)] = total.astype(jnp.bfloat16)

        tiles(p, phase, half, body)

    for phase in (2, 1, 0):
        started = []
        for k in range(2):
            for p in range(3):
                for way in range(2):
                    op = push(p, phase, way, k)
                    op.start()
                    started.append(op)
        for p in range(3):
            m = here[PARTS[p][0][phase]]
            for way in range(2):
                push(p, phase, way, 0).wait_recv()
                add_into(p, phase, hop(m, (1, 3)[way]), way, [(buf(p, phase, way), False)])
                op = push(p, phase, way, 2)
                op.start()
                started.append(op)
        for p in range(3):
            m = here[PARTS[p][0][phase]]
            for way in range(2):
                push(p, phase, way, 1).wait_recv()
                push(p, phase, way, 2).wait_recv()
            add_into(
                p, phase, m, None, [(buf(p, phase, 2), True), (buf(p, phase, 3), True)]
            )
        for op in started:
            op.wait_send()

    total = acc[y, z, x]
    full[c, z, x] = jnp.where(mask[...] > 0, total, jnp.zeros_like(total))

    plane = (z, x)
    siblings = []

    def to_sibling(p, k, t, core):
        at = (core, *region(PLANE_PARTS[p], 1, plane, t, None))
        return pltpu.make_async_remote_copy(
            src_ref=full.at[at], dst_ref=full.at[at],
            send_sem=sib_send.at[p * 4 + k], recv_sem=sib_recv.at[p * 4 + k],
            device_id=sibling, device_id_type=MESH,
        )

    def on_phase(phase):
        if phase == 1:
            for p in range(2):
                op = to_sibling(p, 0, plane[PLANE_PARTS[p][0][1]], c)
                op.start()
                siblings.append(op)

    count = [1, 1]

    def on_chunk(p, phase, t):
        if phase == 1:
            op = to_sibling(p, count[p], t, c)
            op.start()
            siblings.append(op)
            count[p] += 1

    ring_gather(
        full.at[c], PLANE_PARTS, plane, LABEL[:2], (), g_send, g_recv, None, on_phase, on_chunk
    )
    for op in siblings:
        op.wait_send()
    for p in range(2):
        m = plane[PLANE_PARTS[p][0][1]]
        for k, t in enumerate((m, hop(m, 3), hop(m, 1), hop(m, 2))):
            to_sibling(p, k, t, 1 - c).wait_recv()

    docs = docs_ref[...]

    def last(q, carry):
        at = (lax.div(q, 4), lax.rem(q, 4))
        grads = [
            jnp.concatenate(
                [full[(half, *at, pl.ds(blk * HALF, HALF), slice(None))] for half in range(2)], axis=0
            )
            for blk in range(4)
        ]
        out_ref[:, pl.ds(pl.multiple_of(q * 512, 512), 512)] = jnp.dot(
            docs, jnp.concatenate(grads, axis=1), preferred_element_type=jnp.float32
        ).astype(jnp.bfloat16)
        return carry

    lax.fori_loop(0, 16, last, 0)


def reduce_blocks(table, gp, hid, docs_t):
    received = []
    for order, _, rows in PARTS:
        cut = rows // 32 * 16
        for phase in range(3):
            whole = [4] * phase + [rows, BLK]
            dims = sorted(order[:phase])
            for half in range(2):
                part = list(whole)
                if phase == 0:
                    part[0] = (rows - cut, cut)[half]
                else:
                    part[dims.index(order[phase - 1])] = 2
                received.append(pltpu.VMEM(tuple(part), jnp.bfloat16))
            received.extend([pltpu.VMEM(tuple(whole), jnp.bfloat16)] * 2)
    return pl.pallas_call(
        reduce_kernel,
        out_shape=jax.ShapeDtypeStruct((32, 8192), jnp.bfloat16),
        in_specs=[
            pl.BlockSpec(memory_space=pltpu.SMEM),
            pl.BlockSpec(memory_space=pl.ANY),
            pl.BlockSpec(memory_space=pl.ANY),
            pl.BlockSpec(memory_space=pltpu.VMEM),
        ],
        out_specs=pl.BlockSpec(memory_space=pltpu.VMEM),
        scratch_shapes=[
            pltpu.VMEM((POOL + 1, HALF, BLK), jnp.bfloat16),
            pltpu.VMEM((POOL + 1, HALF, BLK), jnp.bfloat16),
            pltpu.VMEM((4, 4, 4, SHARD, BLK), jnp.bfloat16),
            pltpu.VMEM((SHARD, BLK), jnp.bfloat16),
            pltpu.VMEM((2, 4, 4, SHARD, BLK), jnp.bfloat16),
            *received,
            pltpu.SemaphoreType.DMA((3,)),
            pltpu.SemaphoreType.DMA((4,)),
            pltpu.SemaphoreType.DMA((54,)),
            pltpu.SemaphoreType.DMA((54,)),
            pltpu.SemaphoreType.DMA((24,)),
            pltpu.SemaphoreType.DMA((24,)),
            pltpu.SemaphoreType.DMA((8,)),
            pltpu.SemaphoreType.DMA((8,)),
        ],
        compiler_params=pltpu.CompilerParams(
            collective_id=1, has_side_effects=True, vmem_limit_bytes=48 * MIB
        ),
        name="reduce_blocks",
    )(table, gp, hid, docs_t)


def on_device(documents, expand_weight, sparse_weight, feature_lists, positives):
    core = lax.axis_index("label_2")
    group = lax.axis_index(AXES)
    docs_t = documents.T
    hid = expand(jnp.pad(docs_t, ((0, 0), (0, 256 - DOCS))), expand_weight)
    pair = lax.dynamic_slice_in_dim(feature_lists, (group - core) * LBLK_DEV, 2 * LBLK_DEV, 0)
    pair = pair.reshape(2, LBLK_DEV * SLOTS)
    order = lax.sort(pair * 512 + jnp.arange(LBLK_DEV * SLOTS, dtype=jnp.int32)[None, :], dimension=1)
    blocks = order[:, ::NAMED] // 512
    own = lax.dynamic_index_in_dim(order, core, 0, keepdims=False)
    spots = jnp.arange(POOL, dtype=jnp.int32)[None, :, None] - POOL
    match = blocks[:, :, None] == jnp.arange(FBLOCKS, dtype=jnp.int32)[None, None, :]
    table = POOL + jnp.sum(jnp.where(match, spots, 0), axis=1)
    table = jnp.where(core == 0, table, table[::-1]).reshape(-1)
    grad_sparse, gp = label_blocks(
        lax.dynamic_index_in_dim(pair, core, 0, keepdims=False),
        lax.dynamic_index_in_dim(blocks, core, 0, keepdims=False),
        own % 512,
        (group * LBLK_DEV).astype(jnp.int32).reshape(1),
        positives,
        hid.reshape(FBLOCKS, DOCS, BLK),
        sparse_weight,
    )
    grad_expand = reduce_blocks(table, gp, hid, docs_t)
    return (grad_expand, grad_sparse)


def solution(mesh):
    finer = Mesh(mesh.devices.reshape(mesh.shape["feat"], 4, 4, 2), AXES)
    return jax.shard_map(
        on_device,
        mesh=finer,
        in_specs=(P(None, LABEL), P(LABEL, "feat"), P(AXES, None, None, None), P(), P()),
        out_specs=(P(LABEL, "feat"), P(AXES, None, None, None)),
        check_vma=False,
    )
```

time: 500 us -> 200 us (0.40)
  waiting for transfers between devices: 193 us -> 0 us
  Pallas kernels: 0 us -> 175 us
  other arithmetic: 137 us -> 0.74 us
  local copies, waits for them, and re-layouts: 56.9 us -> 10.2 us
  matrix products: 42.3 us -> 0 us
  starting transfers between devices: 28.5 us -> 0 us
  blocking collectives: 25.2 us -> 0 us
    pallas_call x0 -> x3, Pallas kernels: none -> 175 us  [the longest x1 61.8 us: reduce_blocks(): pl.pallas_call(reduce_kernel, out_shape=jax.ShapeDtypeStruct((32, 8192),...]
    all_to_all x5 -> x0, waiting for transfers between devices: 111 us -> none  [the longest x1 42.1 us: on_device(): lax.all_to_all(group_part, 'feat', split_axis=0, concat_axis=0, tiled=True)]
    scatter-add x2 -> x0, other arithmetic: 110 us -> none  [the longest x1 87.4 us: on_device(): jax.ops.segment_sum(back_rows, slot_position.reshape(-1), num_segments=fe...]
    reduce_scatter x1 -> x0, waiting for transfers between devices: 81.8 us -> none  [on_device(): lax.psum_scatter(flat_grad.astype(jnp.bfloat16), LABEL, scatter_dimension...]
    dot_general x5 -> x0, matrix products: 42.3 us -> none  [the longest x1 15.2 us: on_device(): jnp.einsum('dle,lsce->lsdc', residual, sparse_weight, preferred_element_t...]
    gather x17 -> x0, local copies, waits for them, and re-layouts: 29.4 us -> none  [the longest x1 14.8 us: on_device(): jnp.take(incoming.reshape(feat_count * CAP, doc_count, BLK), slot_positio...]
    all_to_all x5 -> x0, starting transfers between devices: 28.2 us -> none  [the longest x2 13.8 us: from_everyone(): return lax.all_to_all(copies, axis, split_axis=0, concat_axis=0, tiled=True)]
    all_to_all x3 -> x0, blocking collectives: 25.2 us -> none  [exchange_in_order(): whole = lax.all_to_all(whole, axes[k], k, k, tiled=True)]
  transfers between devices with their start and end apart: 6 -> 0, of which waited for: 5 -> 0; matrix products, arithmetic and copies ran while one was open for 7% -> 0% of each run, Pallas kernels for 0% -> 0%
where the time goes in v1:
time: 200 us
  Pallas kernels  175 us (88%)
  between operations  14.2 us (7%)
  local copies, waits for them, and re-layouts  10.2 us (5%)
    pallas_call x1, Pallas kernels, reduce_blocks(): pl.pallas_call(reduce_kernel, out_shape=jax.ShapeDtypeStruct((32, 8192),...  61.8 us
    pallas_call x1, Pallas kernels, expand(): pl.pallas_call(expand_kernel, out_shape=jax.ShapeDtypeStruct((4, 4, 4, 2,...  61.1 us
    pallas_call x1, Pallas kernels, label_blocks(): pl.pallas_call(label_kernel, out_shape=(jax.ShapeDtypeStruct((LBLK_DEV, S...  51.6 us
    unnamed x12, local copies, waits for them, and re-layouts  7.5 us

profile of v1, /device:TPU:1, one launch (start us, length us, event | category | flops | bytes accessed | tf_op | source)
XLA Modules:
  0.0 199.6 jit_solution(665877166946134088)
XLA Ops:
  7.2 0.0 copy-start
  7.2 0.0 sort.9.cloned.1.call-start
  7.2 0.9 copy-done
  8.1 0.1 constant_dynamic-slice_fusion.1
  8.2 0.1 copy.10
  8.3 0.1 reshape.22
  8.3 0.6 iota_add_fusion
  8.9 0.0 sort.9.cloned.1.call-update
  9.0 0.8 copy.11.pos_ref
  9.8 0.7 pad.4.docs_ref
  10.5 0.0 copy-start.2
  10.5 1.0 copy-done.2
  11.5 61.1 %expand.1.hid_ref = bf16[4,4,4,2,320,128]{5,4,3,2,1,0:T(8,128)(2,1)S(1)} custom-call(bf16[32,256]{1,0:T(8,128)(2,1)S(1)} %pad.4.docs_ref, bf16[32,8192]{1,0:T(8,128)(2,1)S(1)} %copy-done.2), custom_call_target="tpu_custom_call" | custom-call | tf_op jit(solution)/shard_map/expand/pallas_call | solution.py:230
  72.7 0.0 copy-start.1
  72.7 4.0 %copy-done.1 = bf16[4,4,4,2,320,128]{5,4,3,2,1,0:T(8,128)(2,1)} copy-done((bf16[4,4,4,2,320,128]{5,4,3,2,1,0:T(8,128)(2,1)}, bf16[4,4,4,2,320,128]{5,4,3,2,1,0:T(8,128)(2,1)S(1)}, u32[]{:S(2)}) %copy-start.1) | copy-done | bytes 10485784
  76.6 0.0 copy-start.3
  76.6 0.9 slice.3
  77.6 0.7 dynamic-slice_reduce_fusion
  78.3 0.1 select_reduce_fusion
  78.4 0.1 reverse.3
  78.5 51.6 %label_blocks.1 = (bf16[24,16,128,128]{3,2,1,0:T(8,128)(2,1)}, bf16[96,160,128]{2,1,0:T(8,128)(2,1)S(1)}) custom-call(s32[384]{0:T(512)S(1)} %get-tuple-element.7.lists, s32[96]{0:T(128)S(1)} %fusion.1.blocks, s32[384]{0:T(512)S(1)} %add_select_fusion.named, s32[1]{0:T(128)} %bitcast.1.base, s32[160,8]{1,0:T(8,128)S(1)} %copy.11.pos_ref, ...), custom_call_target="tpu_custom_call" | custom-call | tf_op jit(solution)/shard_map/label_blocks/pallas_call | solution.py:337
  130.1 0.0 copy-done.3
  130.1 61.8 %reduce_blocks.1 = bf16[32,8192]{1,0:T(8,128)(2,1)S(1)} custom-call(s32[512]{0:T(512)S(1)} %bitcast.11, bf16[96,160,128]{2,1,0:T(8,128)(2,1)S(1)} %get-tuple-element.4.gp_ref, bf16[4,4,4,2,320,128]{5,4,3,2,1,0:T(8,128)(2,1)} %copy-done.1, bf16[32,160]{1,0:T(8,128)(2,1)S(1)} %bitcast.10), custom_call_target="tpu_custom_call" | custom-call | tf_op jit(solution)/shard_map/reduce_blocks/pallas_call | solution.py:596
  192.0 0.8 copy.14
  (7 shorter events, 0.0 us)
Async XLA Ops:
  7.2 0.9 copy-start
  7.2 69.5 %sort.9.cloned.1.call-start = ((), (), s32[]{:S(2)}) async-start(), calls=%async_computation | async-start | bytes 9248 | tf_op jit(solution)/shard_map/sort | solution.py:636
  10.5 1.0 copy-start.2
  72.7 4.0 %copy-start.1 = (bf16[4,4,4,2,320,128]{5,4,3,2,1,0:T(8,128)(2,1)}, bf16[4,4,4,2,320,128]{5,4,3,2,1,0:T(8,128)(2,1)S(1)}, u32[]{:S(2)}) copy-start(bf16[4,4,4,2,320,128]{5,4,3,2,1,0:T(8,128)(2,1)S(1)} %expand.1.hid_ref) | copy-start | bytes 31457284
  76.6 53.5 %copy-start.3 = (bf16[160,32]{0,1:T(8,128)(2,1)S(1)}, bf16[160,32]{0,1:T(8,128)(2,1)}, u32[]{:S(2)}) copy-start(bf16[160,32]{0,1:T(8,128)(2,1)} %param.5) | copy-start | bytes 30724
Sparse Core Ops, SparseCore 0:
  10.9 3.0 sort.11.cloned.1.call-done
  (1 shorter events, 0.0 us)

commit v2 on v1

--- a/solution.py
+++ b/solution.py
@@ -13,6 +13,7 @@
 SLOTS = 16
 LBLK_DEV = 24
 POOL = 96
+STEP = 4
 NAMED = 4
 POS = 8
 DOCS = 160
@@ -25,11 +26,18 @@
 MIB = 1 << 20
 
 PARTS = (((2, 0, 1), 0, 112), ((0, 1, 2), 112, 112), ((1, 2, 0), 224, 96))
-PLANE_PARTS = (((0, 1), 0, 160), ((1, 0), 160, 160))
 
 
 def hop(m, k):
     return lax.rem(m + k, RING)
+
+
+def label_peer(l):
+    return {
+        "label_0": lax.div(l, 8),
+        "label_1": lax.rem(lax.div(l, 2), 4),
+        "label_2": lax.rem(l, 2),
+    }
 
 
 def region(part, phase, here, t, half, lead=()):
@@ -61,9 +69,9 @@
             device_id_type=MESH,
         )
 
+    started = []
     for phase in range(len(axes)):
         source = first_source if phase == 0 else None
-        started = []
         for k in range(2):
             for p in range(len(parts)):
                 m = here[parts[p][0][phase]]
@@ -91,25 +99,19 @@
             for way in range(2):
                 copy(p, phase, way, 2, hop(m, 2), way).wait_recv()
             on_chunk(p, phase, hop(m, 2))
-        for op in started:
-            op.wait_send()
+    for op in started:
+        op.wait_send()
 
 
 def expand_kernel(
-    docs_ref, weight_ref, hid_ref, docs_all, w_all, shard,
+    docs_ref, weight_ref, hid_ref, docs_all, mask_ref, w_all, shard,
     w_send, w_recv, d_send, d_recv, own_sem, send, recv, sib_send, sib_recv,
 ):
     y, z, x, c = (lax.axis_index(a) for a in AXES)
     me = z * 8 + x * 2 + c
     sibling = {"label_2": 1 - c}
 
-    def peer(l):
-        return {
-            "label_0": lax.div(l, 8),
-            "label_1": lax.rem(lax.div(l, 2), 4),
-            "label_2": lax.rem(l, 2),
-        }
-
+    peer = label_peer
     barrier = pltpu.get_barrier_semaphore()
 
     def greet(o, carry):
@@ -124,7 +126,7 @@
     pl.semaphore_wait(barrier, 33)
 
     def rows_of(ref, l):
-        return ref.at[pl.ds(pl.multiple_of(l * 32, 32), 32), :]
+        return ref.at[lax.div(l, 2), lax.rem(l, 2)]
 
     def columns_for(l):
         return weight_ref.at[:, pl.ds(pl.multiple_of(l * 256, 256), 256)]
@@ -136,6 +138,13 @@
             device_id=peer(to), device_id_type=MESH,
         )
 
+    def docs_pair(core):
+        return pltpu.make_async_remote_copy(
+            src_ref=docs_all.at[:, core], dst_ref=docs_all.at[:, core],
+            send_sem=own_sem.at[3], recv_sem=own_sem.at[4],
+            device_id=sibling, device_id_type=MESH,
+        )
+
     def weight_copy(to, origin):
         return pltpu.make_async_remote_copy(
             src_ref=columns_for(to), dst_ref=rows_of(w_all, origin),
@@ -143,13 +152,19 @@
             device_id=peer(to), device_id_type=MESH,
         )
 
-    def start(o, carry):
-        to = lax.rem(me + o, 32)
-        weight_copy(to, me).start()
-        docs_copy(to, me).start()
-        return carry
-
-    lax.fori_loop(1, 32, start, 0)
+    def same_core(o):
+        return lax.rem(me + 2 * o, 32)
+
+    def start_docs(o, carry):
+        docs_copy(same_core(o), me).start()
+        return carry
+
+    def start_weight(o, carry):
+        weight_copy(lax.rem(me + o, 32), me).start()
+        return carry
+
+    lax.fori_loop(1, 16, start_docs, 0)
+    lax.fori_loop(1, 32, start_weight, 0)
     own_docs = pltpu.make_async_copy(docs_ref, rows_of(docs_all, me), own_sem.at[0])
     own_weight = pltpu.make_async_copy(columns_for(me), rows_of(w_all, me), own_sem.at[1])
     own_docs.start()
@@ -157,15 +172,22 @@
     own_docs.wait()
     own_weight.wait()
 
-    def finish(o, carry):
+    def finish_docs(o, carry):
+        docs_copy(same_core(o), same_core(o)).wait_recv()
+        return carry
+
+    def finish_weight(o, carry):
         other = lax.rem(me + o, 32)
         weight_copy(other, other).wait_recv()
-        docs_copy(other, other).wait_recv()
-        return carry
-
-    lax.fori_loop(1, 32, finish, 0)
+        return carry
+
+    lax.fori_loop(1, 16, finish_docs, 0)
+    docs_pair(c).start()
+    lax.fori_loop(1, 32, finish_weight, 0)
+    docs_pair(1 - c).wait_recv()
     product = lax.dot_general(
-        docs_all[...], w_all[...], (((0,), (0,)), ((), ())), preferred_element_type=jnp.float32
+        docs_all[...].reshape(1024, 256), w_all[...].reshape(1024, 256),
+        (((0,), (0,)), ((), ())), preferred_element_type=jnp.float32,
     )
     hidden = jnp.maximum(product, 0.0).astype(jnp.bfloat16)
     shard[0:DOCS, :] = hidden[:DOCS, :BLK]
@@ -217,37 +239,63 @@
                 device_id=sibling, device_id_type=MESH,
             ).wait_recv()
 
-    def drain(o, carry):
-        to = lax.rem(me + o, 32)
-        weight_copy(to, me).wait_send()
-        docs_copy(to, me).wait_send()
-        return carry
-
-    lax.fori_loop(1, 32, drain, 0)
+    docs_pair(c).wait_send()
+    for blk in range(4):
+        op = pltpu.make_async_copy(
+            hid_ref.at[
+                y, z, x, blk // 2,
+                pl.ds(pl.multiple_of(blk % 2 * DOCS + c * HALF, 16), HALF), slice(None),
+            ],
+            mask_ref.at[pl.ds(blk * HALF, HALF), :],
+            own_sem.at[blk],
+        )
+        op.start()
+    for blk in range(4):
+        pltpu.make_async_copy(
+            mask_ref.at[pl.ds(blk * HALF, HALF), :], mask_ref.at[pl.ds(blk * HALF, HALF), :], own_sem.at[blk]
+        ).wait()
+
+    def drain_docs(o, carry):
+        docs_copy(same_core(o), me).wait_send()
+        return carry
+
+    def drain_weight(o, carry):
+        weight_copy(lax.rem(me + o, 32), me).wait_send()
+        return carry
+
+    lax.fori_loop(1, 16, drain_docs, 0)
+    lax.fori_loop(1, 32, drain_weight, 0)
 
 
 def expand(docs_t, expand_weight):
     return pl.pallas_call(
         expand_kernel,
-        out_shape=jax.ShapeDtypeStruct((4, 4, 4, 2, SHARD, BLK), jnp.bfloat16),
+        out_shape=(
+            jax.ShapeDtypeStruct((4, 4, 4, 2, SHARD, BLK), jnp.bfloat16),
+            jax.ShapeDtypeStruct((16, 2, 32, 256), jnp.bfloat16),
+            jax.ShapeDtypeStruct((SHARD, BLK), jnp.bfloat16),
+        ),
         in_specs=[pl.BlockSpec(memory_space=pltpu.VMEM), pl.BlockSpec(memory_space=pl.ANY)],
-        out_specs=pl.BlockSpec(memory_space=pl.ANY),
+        out_specs=(
+            pl.BlockSpec(memory_space=pl.ANY),
+            pl.BlockSpec(memory_space=pltpu.VMEM),
+            pl.BlockSpec(memory_space=pltpu.VMEM),
+        ),
         scratch_shapes=[
-            pltpu.VMEM((1024, 256), jnp.bfloat16),
-            pltpu.VMEM((1024, 256), jnp.bfloat16),
+            pltpu.VMEM((16, 2, 32, 256), jnp.bfloat16),
             pltpu.VMEM((SHARD, BLK), jnp.bfloat16),
             pltpu.SemaphoreType.DMA((32,)),
             pltpu.SemaphoreType.DMA((32,)),
             pltpu.SemaphoreType.DMA((32,)),
             pltpu.SemaphoreType.DMA((32,)),
-            pltpu.SemaphoreType.DMA((3,)),
+            pltpu.SemaphoreType.DMA((5,)),
             pltpu.SemaphoreType.DMA((54,)),
             pltpu.SemaphoreType.DMA((54,)),
             pltpu.SemaphoreType.DMA((12,)),
             pltpu.SemaphoreType.DMA((12,)),
         ],
         compiler_params=pltpu.CompilerParams(
-            collective_id=0, has_side_effects=True, vmem_limit_bytes=16 * MIB
+            collective_id=0, has_side_effects=True, vmem_limit_bytes=36 * MIB
         ),
         name="expand",
     )(docs_t, expand_weight)
@@ -288,32 +336,41 @@
             h_t[p] = h[p].T
             return carry
 
-        lax.fori_loop(0, POOL, arrive, 0)
-
-    weight_copy(g).wait()
-    where = [place[lists[g * SLOTS + s]] for s in range(SLOTS)]
-    logits = jnp.zeros((DOCS, BLK), jnp.float32)
-    for s in range(0, SLOTS, 2):
-        left = jnp.concatenate([h[where[s]], h[where[s + 1]]], axis=1)
-        right = w[g, s : s + 2].reshape(2 * BLK, BLK)
-        logits += jnp.dot(left, right, preferred_element_type=jnp.float32)
-    ids = (base[0] + g) * BLK + lax.broadcasted_iota(jnp.int32, (DOCS, BLK), 1)
-    hit = pos_b[0] == ids
-    for k in range(1, POS):
-        hit = jnp.logical_or(hit, pos_b[k] == ids)
-    residual = (jax.nn.sigmoid(logits) - jnp.where(hit, 1.0, 0.0)).astype(jnp.bfloat16)
-    res[g] = residual
-    for s in range(SLOTS):
-        gs_ref[0, s] = jnp.dot(
-            h_t[where[s]], residual, preferred_element_type=jnp.float32
-        ).astype(jnp.bfloat16)
+        lax.fori_loop(0, POOL, arrive, 0, unroll=8)
+
+    rows = [g * STEP + k for k in range(STEP)]
+    spots = [[place[lists[q * SLOTS + s]] for s in range(SLOTS)] for q in rows]
+    for q in rows:
+        weight_copy(q).wait()
+    scores = []
+    for q, where in zip(rows, spots):
+        logits = jnp.zeros((DOCS, BLK), jnp.float32)
+        for s in range(0, SLOTS, 2):
+            left = jnp.concatenate([h[where[s]], h[where[s + 1]]], axis=1)
+            right = w[q, s : s + 2].reshape(2 * BLK, BLK)
+            logits += jnp.dot(left, right, preferred_element_type=jnp.float32)
+        scores.append(logits)
+    residuals = []
+    for q, logits in zip(rows, scores):
+        ids = (base[0] + q) * BLK + lax.broadcasted_iota(jnp.int32, (DOCS, BLK), 1)
+        hit = pos_b[0] == ids
+        for k in range(1, POS):
+            hit = jnp.logical_or(hit, pos_b[k] == ids)
+        residual = (jax.nn.sigmoid(logits) - jnp.where(hit, 1.0, 0.0)).astype(jnp.bfloat16)
+        res[q] = residual
+        residuals.append(residual)
+    for k, (where, residual) in enumerate(zip(spots, residuals)):
+        for s in range(SLOTS):
+            gs_ref[k, s] = jnp.dot(
+                h_t[where[s]], residual, preferred_element_type=jnp.float32
+            ).astype(jnp.bfloat16)
 
     def gp_copy(f):
         return pltpu.make_async_copy(
             gp.at[pl.ds(f * 24, 24)], gp_ref.at[pl.ds(f * 24, 24)], gp_sem.at[f]
         )
 
-    @pl.when(g == LBLK_DEV - 1)
+    @pl.when(g == LBLK_DEV // STEP - 1)
     def _():
         for f in range(4):
 
@@ -327,7 +384,7 @@
                 ).astype(jnp.bfloat16)
                 return carry
 
-            lax.fori_loop(f * 24, f * 24 + 24, collect, 0)
+            lax.fori_loop(f * 24, f * 24 + 24, collect, 0, unroll=8)
             gp_copy(f).start()
         for f in range(4):
             gp_copy(f).wait()
@@ -342,14 +399,14 @@
         ),
         grid_spec=pltpu.PrefetchScalarGridSpec(
             num_scalar_prefetch=4,
-            grid=(LBLK_DEV,),
+            grid=(LBLK_DEV // STEP,),
             in_specs=[
                 pl.BlockSpec((DOCS, POS), lambda g, *_: (0, 0)),
                 pl.BlockSpec(memory_space=pl.ANY),
                 pl.BlockSpec(memory_space=pl.ANY),
             ],
             out_specs=(
-                pl.BlockSpec((1, SLOTS, BLK, BLK), lambda g, *_: (g, 0, 0, 0)),
+                pl.BlockSpec((STEP, SLOTS, BLK, BLK), lambda g, *_: (g, 0, 0, 0)),
                 pl.BlockSpec(memory_space=pl.ANY),
             ),
             scratch_shapes=[
@@ -366,26 +423,32 @@
             ],
         ),
         compiler_params=pltpu.CompilerParams(
-            dimension_semantics=("arbitrary",), vmem_limit_bytes=48 * MIB
+            dimension_semantics=("arbitrary",), vmem_limit_bytes=36 * MIB
         ),
         name="label_blocks",
     )(lists, blocks, named, base, positives, hid, sparse_weight)
 
 
 def reduce_kernel(
-    table, gp_ref, hid_ref, docs_ref, out_ref,
-    own, sib, acc, mask, full, *rest,
+    table, gp_ref, mask, docs_ref, out_ref,
+    own, sib, acc, grad, mine_grad, pieces, *rest,
 ):
-    bufs, (pair_sem, mask_sem, send, recv, g_send, g_recv, sib_send, sib_recv) = rest[:36], rest[36:]
+    bufs, (pair_sem, mask_sem, send, recv, o_send, o_recv) = rest[:36], rest[36:]
     y, z, x, c = (lax.axis_index(a) for a in AXES)
     here = (y, z, x)
     sibling = {"label_2": 1 - c}
+    me = z * 8 + x * 2 + c
     barrier = pltpu.get_barrier_semaphore()
-    for axis, m in zip(AXES, here):
-        for k in (1, 3):
-            pl.semaphore_signal(barrier, inc=1, device_id={axis: hop(m, k)}, device_id_type=MESH)
-    pl.semaphore_signal(barrier, inc=1, device_id=sibling, device_id_type=MESH)
-    pl.semaphore_wait(barrier, 7)
+
+    def greet(o, carry):
+        pl.semaphore_signal(
+            barrier, inc=1, device_id=label_peer(lax.rem(me + o, 32)), device_id_type=MESH
+        )
+        return carry
+
+    lax.fori_loop(1, 32, greet, 0)
+    for k in (1, 3):
+        pl.semaphore_signal(barrier, inc=1, device_id={"feat": hop(y, k)}, device_id_type=MESH)
 
     def docs_half(k):
         return gp_ref.at[:, pl.ds(pl.multiple_of(k * HALF, 16), HALF), :]
@@ -395,24 +458,14 @@
         send_sem=pair_sem.at[0], recv_sem=pair_sem.at[1],
         device_id=sibling, device_id_type=MESH,
     )
-    to_pair.start()
     mine = pltpu.make_async_copy(docs_half(c), own.at[pl.ds(0, POOL)], pair_sem.at[2])
     mine.start()
-    masks = []
-    for blk in range(4):
-        op = pltpu.make_async_copy(
-            hid_ref.at[y, z, x, blk // 2, pl.ds(pl.multiple_of(blk % 2 * DOCS + c * HALF, 16), HALF), :],
-            mask.at[pl.ds(blk * HALF, HALF), :],
-            mask_sem.at[blk],
-        )
-        op.start()
-        masks.append(op)
     own[POOL] = jnp.zeros((HALF, BLK), jnp.bfloat16)
     sib[POOL] = jnp.zeros((HALF, BLK), jnp.bfloat16)
+    pl.semaphore_wait(barrier, 33)
+    to_pair.start()
     mine.wait()
     to_pair.wait()
-    for op in masks:
-        op.wait()
 
     def spread(q, carry):
         at = (lax.div(q, 16), lax.rem(lax.div(q, 4), 4), lax.rem(q, 4))
@@ -493,8 +546,8 @@
 
         tiles(p, phase, half, body)
 
+    started = []
     for phase in (2, 1, 0):
-        started = []
         for k in range(2):
             for p in range(3):
                 for way in range(2):
@@ -517,68 +570,76 @@
             add_into(
                 p, phase, m, None, [(buf(p, phase, 2), True), (buf(p, phase, 3), True)]
             )
-        for op in started:
-            op.wait_send()
 
     total = acc[y, z, x]
-    full[c, z, x] = jnp.where(mask[...] > 0, total, jnp.zeros_like(total))
-
-    plane = (z, x)
-    siblings = []
-
-    def to_sibling(p, k, t, core):
-        at = (core, *region(PLANE_PARTS[p], 1, plane, t, None))
+    grad[...] = jnp.where(mask[...] > 0, total, jnp.zeros_like(total))
+
+    def columns(k):
+        return grad.at[pl.ds(pl.multiple_of(k * DOCS, 16), DOCS), :]
+
+    def pair_grad(k, core):
         return pltpu.make_async_remote_copy(
-            src_ref=full.at[at], dst_ref=full.at[at],
-            send_sem=sib_send.at[p * 4 + k], recv_sem=sib_recv.at[p * 4 + k],
+            src_ref=columns(k), dst_ref=mine_grad.at[core],
+            send_sem=pair_sem.at[3], recv_sem=pair_sem.at[4],
             device_id=sibling, device_id_type=MESH,
         )
 
-    def on_phase(phase):
-        if phase == 1:
-            for p in range(2):
-                op = to_sibling(p, 0, plane[PLANE_PARTS[p][0][1]], c)
-                op.start()
-                siblings.append(op)
-
-    count = [1, 1]
-
-    def on_chunk(p, phase, t):
-        if phase == 1:
-            op = to_sibling(p, count[p], t, c)
-            op.start()
-            siblings.append(op)
-            count[p] += 1
-
-    ring_gather(
-        full.at[c], PLANE_PARTS, plane, LABEL[:2], (), g_send, g_recv, None, on_phase, on_chunk
-    )
-    for op in siblings:
+    to_other = pair_grad(1 - c, c)
+    to_other.start()
+    kept = pltpu.make_async_copy(columns(c), mine_grad.at[c], pair_sem.at[5])
+    kept.start()
+    kept.wait()
+    pair_grad(c, 1 - c).wait_recv()
+    sides = [
+        jnp.concatenate([mine_grad[half, pl.ds(j * HALF, HALF), :] for half in range(2)], axis=0)
+        for j in range(2)
+    ]
+    right = jnp.concatenate(sides, axis=1)
+
+    def out_columns(l):
+        return out_ref.at[:, pl.ds(pl.multiple_of(l * 256, 256), 256)]
+
+    def out_copy(to, origin):
+        return pltpu.make_async_remote_copy(
+            src_ref=pieces.at[to], dst_ref=out_columns(origin),
+            send_sem=o_send.at[to], recv_sem=o_recv.at[origin],
+            device_id=label_peer(to), device_id_type=MESH,
+        )
+
+    own_out = pltpu.make_async_copy(pieces.at[me], out_columns(me), pair_sem.at[6])
+    for k in range(4):
+        row = hop(z, k) * 8
+        left = docs_ref[pl.ds(hop(z, k) * 4, 4)].reshape(256, 256)[:, :DOCS]
+        pieces[pl.ds(row, 8)] = jnp.dot(
+            left, right, preferred_element_type=jnp.float32
+        ).astype(jnp.bfloat16).reshape(8, 32, 256)
+
+        def deliver(o, carry):
+            out_copy(row + lax.rem(x * 2 + c + o, 8), me).start()
+            return carry
+
+        lax.fori_loop(1 if k == 0 else 0, 8, deliver, 0)
+        if k == 0:
+            own_out.start()
+    own_out.wait()
+
+    def collect(o, carry):
+        other = lax.rem(me + o, 32)
+        out_copy(other, other).wait_recv()
+        return carry
+
+    def drain(o, carry):
+        out_copy(lax.rem(me + o, 32), me).wait_send()
+        return carry
+
+    lax.fori_loop(1, 32, collect, 0)
+    to_other.wait_send()
+    for op in started:
         op.wait_send()
-    for p in range(2):
-        m = plane[PLANE_PARTS[p][0][1]]
-        for k, t in enumerate((m, hop(m, 3), hop(m, 1), hop(m, 2))):
-            to_sibling(p, k, t, 1 - c).wait_recv()
-
-    docs = docs_ref[...]
-
-    def last(q, carry):
-        at = (lax.div(q, 4), lax.rem(q, 4))
-        grads = [
-            jnp.concatenate(
-                [full[(half, *at, pl.ds(blk * HALF, HALF), slice(None))] for half in range(2)], axis=0
-            )
-            for blk in range(4)
-        ]
-        out_ref[:, pl.ds(pl.multiple_of(q * 512, 512), 512)] = jnp.dot(
-            docs, jnp.concatenate(grads, axis=1), preferred_element_type=jnp.float32
-        ).astype(jnp.bfloat16)
-        return carry
-
-    lax.fori_loop(0, 16, last, 0)
-
-
-def reduce_blocks(table, gp, hid, docs_t):
+    lax.fori_loop(1, 32, drain, 0)
+
+
+def reduce_blocks(table, gp, mask, docs_all):
     received = []
     for order, _, rows in PARTS:
         cut = rows // 32 * 16
@@ -599,7 +660,7 @@
         in_specs=[
             pl.BlockSpec(memory_space=pltpu.SMEM),
             pl.BlockSpec(memory_space=pl.ANY),
-            pl.BlockSpec(memory_space=pl.ANY),
+            pl.BlockSpec(memory_space=pltpu.VMEM),
             pl.BlockSpec(memory_space=pltpu.VMEM),
         ],
         out_specs=pl.BlockSpec(memory_space=pltpu.VMEM),
@@ -608,29 +669,28 @@
             pltpu.VMEM((POOL + 1, HALF, BLK), jnp.bfloat16),
             pltpu.VMEM((4, 4, 4, SHARD, BLK), jnp.bfloat16),
             pltpu.VMEM((SHARD, BLK), jnp.bfloat16),
-            pltpu.VMEM((2, 4, 4, SHARD, BLK), jnp.bfloat16),
+            pltpu.VMEM((2, DOCS, BLK), jnp.bfloat16),
+            pltpu.VMEM((32, 32, 256), jnp.bfloat16),
             *received,
-            pltpu.SemaphoreType.DMA((3,)),
+            pltpu.SemaphoreType.DMA((7,)),
             pltpu.SemaphoreType.DMA((4,)),
             pltpu.SemaphoreType.DMA((54,)),
             pltpu.SemaphoreType.DMA((54,)),
-            pltpu.SemaphoreType.DMA((24,)),
-            pltpu.SemaphoreType.DMA((24,)),
-            pltpu.SemaphoreType.DMA((8,)),
-            pltpu.SemaphoreType.DMA((8,)),
+            pltpu.SemaphoreType.DMA((32,)),
+            pltpu.SemaphoreType.DMA((32,)),
         ],
         compiler_params=pltpu.CompilerParams(
-            collective_id=1, has_side_effects=True, vmem_limit_bytes=48 * MIB
+            collective_id=1, has_side_effects=True, vmem_limit_bytes=24 * MIB
         ),
         name="reduce_blocks",
-    )(table, gp, hid, docs_t)
+    )(table, gp, mask, docs_all)
 
 
 def on_device(documents, expand_weight, sparse_weight, feature_lists, positives):
     core = lax.axis_index("label_2")
     group = lax.axis_index(AXES)
     docs_t = documents.T
-    hid = expand(jnp.pad(docs_t, ((0, 0), (0, 256 - DOCS))), expand_weight)
+    hid, docs_all, mask = expand(jnp.pad(docs_t, ((0, 0), (0, 256 - DOCS))), expand_weight)
     pair = lax.dynamic_slice_in_dim(feature_lists, (group - core) * LBLK_DEV, 2 * LBLK_DEV, 0)
     pair = pair.reshape(2, LBLK_DEV * SLOTS)
     order = lax.sort(pair * 512 + jnp.arange(LBLK_DEV * SLOTS, dtype=jnp.int32)[None, :], dimension=1)
@@ -649,7 +709,7 @@
         hid.reshape(FBLOCKS, DOCS, BLK),
         sparse_weight,
     )
-    grad_expand = reduce_blocks(table, gp, hid, docs_t)
+    grad_expand = reduce_blocks(table, gp, mask, docs_all)
     return (grad_expand, grad_sparse)
 
 

time: 200 us -> 180 us (0.900)
  Pallas kernels: 175 us -> 150 us
  local copies, waits for them, and re-layouts: 10.2 us -> 14.2 us
    pallas_call x1, Pallas kernels: 51.6 us -> 37.5 us  [label_blocks(): pl.pallas_call(label_kernel, out_shape=(jax.ShapeDtypeStruct((LBLK_DEV, S...]
    pallas_call x1, Pallas kernels: 61.8 us -> 55.1 us  [reduce_blocks(): pl.pallas_call(reduce_kernel, out_shape=jax.ShapeDtypeStruct((32, 8192),...]
    unnamed x12, local copies, waits for them, and re-layouts: 7.5 us -> 11.6 us
    pallas_call x1, Pallas kernels: 61.1 us -> 57.7 us  [expand(): pl.pallas_call(expand_kernel, out_shape=(jax.ShapeDtypeStruct((4, 4, 4, 2...]
where the time goes in v2:
time: 180 us; the launch traced here: 179 us
  Pallas kernels  150 us (83%)
  local copies, waits for them, and re-layouts  14.2 us (8%)
  between operations  14.2 us (8%)
    pallas_call x1, Pallas kernels, expand(): pl.pallas_call(expand_kernel, out_shape=(jax.ShapeDtypeStruct((4, 4, 4, 2...  57.7 us
    pallas_call x1, Pallas kernels, reduce_blocks(): pl.pallas_call(reduce_kernel, out_shape=jax.ShapeDtypeStruct((32, 8192),...  55.1 us
    pallas_call x1, Pallas kernels, label_blocks(): pl.pallas_call(label_kernel, out_shape=(jax.ShapeDtypeStruct((LBLK_DEV, S...  37.5 us
    unnamed x12, local copies, waits for them, and re-layouts  11.6 us

profile of v2, /device:TPU:1, one launch (start us, length us, event | category | flops | bytes accessed | tf_op | source)
XLA Modules:
  0.0 179.5 jit_solution(14422966488657309252)
XLA Ops:
  7.2 0.0 copy-start
  7.2 0.0 sort.9.cloned.1.call-start
  7.2 0.9 copy-done
  8.1 0.1 constant_dynamic-slice_fusion.1
  8.2 0.1 copy.10
  8.3 0.1 reshape.22
  8.3 0.6 iota_add_fusion
  8.9 0.0 sort.9.cloned.1.call-update
  9.0 0.8 copy.11.pos_ref
  9.8 0.7 pad.4.docs_ref
  10.5 0.0 copy-start.3
  10.5 1.0 copy-done.3
  11.5 57.7 %expand.1 = (bf16[4,4,4,2,320,128]{5,4,3,2,1,0:T(8,128)(2,1)S(1)}, bf16[16,2,32,256]{3,2,1,0:T(8,128)(2,1)S(1)}, bf16[320,128]{1,0:T(8,128)(2,1)S(1)}) custom-call(bf16[32,256]{1,0:T(8,128)(2,1)S(1)} %pad.4.docs_ref, bf16[32,8192]{1,0:T(8,128)(2,1)S(1)} %copy-done.3), custom_call_target="tpu_custom_call" | custom-call | tf_op jit(solution)/shard_map/expand/pallas_call | solution.py:271
  69.3 0.0 copy-start.1
  69.3 4.1 %copy-done.1 = bf16[4,4,4,2,320,128]{5,4,3,2,1,0:T(8,128)(2,1)} copy-done((bf16[4,4,4,2,320,128]{5,4,3,2,1,0:T(8,128)(2,1)}, bf16[4,4,4,2,320,128]{5,4,3,2,1,0:T(8,128)(2,1)S(1)}, u32[]{:S(2)}) %copy-start.1) | copy-done | bytes 10485784
  73.4 0.7 dynamic-slice_reduce_fusion
  74.1 0.9 slice.3
  75.0 0.1 select_reduce_fusion
  75.1 0.1 reverse.3
  75.2 0.0 copy-start.2
  75.2 4.0 %copy-done.2 = bf16[4,4,4,2,320,128]{5,4,3,2,1,0:T(8,128)(2,1)S(1)} copy-done((bf16[4,4,4,2,320,128]{5,4,3,2,1,0:T(8,128)(2,1)S(1)}, bf16[4,4,4,2,320,128]{5,4,3,2,1,0:T(8,128)(2,1)}, u32[]{:S(2)}) %copy-start.2) | copy-done | bytes 10485784
  79.2 37.5 %label_blocks.1 = (bf16[24,16,128,128]{3,2,1,0:T(8,128)(2,1)}, bf16[96,160,128]{2,1,0:T(8,128)(2,1)S(1)}) custom-call(s32[384]{0:T(512)S(1)} %get-tuple-element.13.lists, s32[96]{0:T(128)S(1)} %fusion.1.blocks, s32[384]{0:T(512)S(1)} %add_select_fusion.named, s32[1]{0:T(128)} %bitcast.1.base, s32[160,8]{1,0:T(8,128)S(1)} %copy.11.pos_ref, ...), custom_call_target="tpu_custom_call" | custom-call | tf_op jit(solution)/shard_map/label_blocks/pallas_call | solution.py:394
  116.7 55.1 %reduce_blocks.1 = bf16[32,8192]{1,0:T(8,128)(2,1)S(1)} custom-call(s32[512]{0:T(512)S(1)} %bitcast.9, bf16[96,160,128]{2,1,0:T(8,128)(2,1)S(1)} %get-tuple-element.8.gp_ref, bf16[320,128]{1,0:T(8,128)(2,1)S(1)} %get-tuple-element.9.mask, bf16[16,2,32,256]{3,2,1,0:T(8,128)(2,1)S(1)} %get-tuple-element.10.docs_ref), custom_call_target="tpu_custom_call" | custom-call | tf_op jit(solution)/shard_map/reduce_blocks/pallas_call | solution.py:657
  171.8 0.8 copy.14
  (7 shorter events, 0.0 us)
Async XLA Ops:
  7.2 0.9 copy-start
  7.2 66.2 %sort.9.cloned.1.call-start = ((), (), s32[]{:S(2)}) async-start(), calls=%async_computation | async-start | bytes 9248 | tf_op jit(solution)/shard_map/sort | solution.py:696
  10.5 1.0 copy-start.3
  69.3 4.1 %copy-start.1 = (bf16[4,4,4,2,320,128]{5,4,3,2,1,0:T(8,128)(2,1)}, bf16[4,4,4,2,320,128]{5,4,3,2,1,0:T(8,128)(2,1)S(1)}, u32[]{:S(2)}) copy-start(bf16[4,4,4,2,320,128]{5,4,3,2,1,0:T(8,128)(2,1)S(1)} %get-tuple-element.7) | copy-start | bytes 31457284
  75.2 4.0 %copy-start.2 = (bf16[4,4,4,2,320,128]{5,4,3,2,1,0:T(8,128)(2,1)S(1)}, bf16[4,4,4,2,320,128]{5,4,3,2,1,0:T(8,128)(2,1)}, u32[]{:S(2)}) copy-start(bf16[4,4,4,2,320,128]{5,4,3,2,1,0:T(8,128)(2,1)} %copy-done.1) | copy-start | bytes 31457284
Sparse Core Ops, SparseCore 0:
  10.9 3.0 sort.11.cloned.1.call-done
  (1 shorter events, 0.0 us)

commit v3 on v2

v3 whole, which is shorter than its diff:
```python
import functools

import jax
import jax.numpy as jnp
from jax import lax
from jax.experimental import pallas as pl
from jax.experimental.pallas import tpu as pltpu
from jax.sharding import Mesh
from jax.sharding import PartitionSpec as P

BLK = 128
FBLOCKS = 256
SLOTS = 16
LBLK_DEV = 24
POOL = 96
STEP = 4
NAMED = 4
POS = 8
DOCS = 160
HALF = 80
SHARD = 320
RING = 4
AXES = ("feat", "label_0", "label_1", "label_2")
LABEL = AXES[1:]
MESH = pl.DeviceIdType.MESH
MIB = 1 << 20

PARTS = (((2, 0, 1), 0, 112), ((0, 1, 2), 112, 112), ((1, 2, 0), 224, 96))
NEAR, BACK = (1, 3, 2), (3, 1, 2)
LINES = (0, 3, 1, 2)


def hop(m, k):
    return lax.rem(m + k, RING)


def label_peer(l):
    return {
        "label_0": lax.div(l, 8),
        "label_1": lax.rem(lax.div(l, 2), 4),
        "label_2": lax.rem(l, 2),
    }


def cell(part, ta, tb, tc, lead=()):
    order, row, rows = part
    index = [None] * 3
    for axis, t in zip(order, (ta, tb, tc)):
        index[axis] = t
    return (*index, *lead, pl.ds(row, rows), slice(None))


def two(half):
    return pl.ds(2 * half, 2)


def rank_tables(keys, tables_ref):
    count = LBLK_DEV * SLOTS
    turned = keys.T
    tables_ref[...] = jnp.zeros((8, count), jnp.int32)
    lanes = lax.broadcasted_iota(jnp.int32, (count, count), 1)
    for r in range(2):
        row, col = keys[r : r + 1, :], turned[:, r : r + 1]
        below = jnp.sum(jnp.where(row < col, 1.0, 0.0), axis=1, keepdims=True).astype(jnp.int32)
        if r == 0:
            sort = jnp.where(below == lanes, col.astype(jnp.float32), 0.0)
            tables_ref[0:1, :] = jnp.sum(sort, axis=0, keepdims=True).astype(jnp.int32)
            above = jnp.sum(jnp.where(col < row, 1.0, 0.0), axis=0, keepdims=True)
            tables_ref[1:2, :] = lax.shift_right_logical(above.astype(jnp.int32), 2)
        place = lax.shift_right_logical(below, 2)
        first = jnp.where(place * NAMED == below, place - POOL, 0).astype(jnp.float32)
        hit = lax.shift_right_logical(col, 9) == lanes[:, :FBLOCKS]
        table = jnp.sum(jnp.where(hit, first, 0.0), axis=0, keepdims=True)
        tables_ref[2 + r : 3 + r, 0:FBLOCKS] = table.astype(jnp.int32) + POOL


def expand_kernel(
    keys_ref, docs_in, weight_ref, hid_ref, docs_all, mask_ref, tables_ref, docs_ref, w_all, shard,
    w_send, w_recv, d_send, d_recv, own_sem, send, recv, sib_send, sib_recv,
):
    y, z, x, c = (lax.axis_index(a) for a in AXES)
    here = (y, z, x)
    me = z * 8 + x * 2 + c
    sibling = {"label_2": 1 - c}
    peer = label_peer
    docs_ref[:, 0:DOCS] = docs_in[...]
    docs_ref[:, DOCS:] = jnp.zeros((32, 256 - DOCS), jnp.bfloat16)
    barrier = pltpu.get_barrier_semaphore()

    def greet(o, carry):
        pl.semaphore_signal(
            barrier, inc=1, device_id=peer(lax.rem(me + o, 32)), device_id_type=MESH
        )
        return carry

    lax.fori_loop(1, 32, greet, 0)
    for k in (1, 2, 3):
        pl.semaphore_signal(barrier, inc=1, device_id={"feat": hop(y, k)}, device_id_type=MESH)
    pl.semaphore_wait(barrier, 34)

    def rows_of(ref, l):
        return ref.at[lax.div(l, 2), lax.rem(l, 2)]

    def columns_for(l):
        return weight_ref.at[:, pl.ds(pl.multiple_of(l * 256, 256), 256)]

    def docs_copy(to, origin):
        return pltpu.make_async_remote_copy(
            src_ref=docs_ref, dst_ref=rows_of(docs_all, origin),
            send_sem=d_send.at[to], recv_sem=d_recv.at[origin],
            device_id=peer(to), device_id_type=MESH,
        )

    def docs_pair(core):
        return pltpu.make_async_remote_copy(
            src_ref=docs_all.at[:, core], dst_ref=docs_all.at[:, core],
            send_sem=own_sem.at[3], recv_sem=own_sem.at[4],
            device_id=sibling, device_id_type=MESH,
        )

    def weight_copy(to, origin):
        return pltpu.make_async_remote_copy(
            src_ref=columns_for(to), dst_ref=rows_of(w_all, origin),
            send_sem=w_send.at[to], recv_sem=w_recv.at[origin],
            device_id=peer(to), device_id_type=MESH,
        )

    def same_core(o):
        return lax.rem(me + 2 * o, 32)

    def start_docs(o, carry):
        docs_copy(same_core(o), me).start()
        return carry

    def start_weight(o, carry):
        weight_copy(lax.rem(me + o, 32), me).start()
        return carry

    lax.fori_loop(1, 16, start_docs, 0)
    lax.fori_loop(1, 32, start_weight, 0)
    own_docs = pltpu.make_async_copy(docs_ref, rows_of(docs_all, me), own_sem.at[0])
    own_weight = pltpu.make_async_copy(columns_for(me), rows_of(w_all, me), own_sem.at[1])
    own_docs.start()
    own_weight.start()
    rank_tables(keys_ref[...], tables_ref)
    own_docs.wait()
    own_weight.wait()

    def finish_docs(o, carry):
        docs_copy(same_core(o), same_core(o)).wait_recv()
        return carry

    def finish_weight(o, carry):
        other = lax.rem(me + o, 32)
        weight_copy(other, other).wait_recv()
        return carry

    lax.fori_loop(1, 16, finish_docs, 0)
    docs_pair(c).start()
    lax.fori_loop(1, 32, finish_weight, 0)
    docs_pair(1 - c).wait_recv()
    product = lax.dot_general(
        docs_all[...].reshape(1024, 256), w_all[...].reshape(1024, 256),
        (((0,), (0,)), ((), ())), preferred_element_type=jnp.float32,
    )
    hidden = jnp.maximum(product, 0.0).astype(jnp.bfloat16)
    shard[0:DOCS, :] = hidden[:DOCS, :BLK]
    shard[DOCS:SHARD, :] = hidden[:DOCS, BLK:]
    own_hidden = pltpu.make_async_copy(shard, hid_ref.at[y, z, x, c], own_sem.at[2])
    own_hidden.start()

    started = []

    def copy(at, slot, axis, k, source=None):
        return pltpu.make_async_remote_copy(
            src_ref=hid_ref.at[at] if source is None else source,
            dst_ref=hid_ref.at[at],
            send_sem=send.at[slot],
            recv_sem=recv.at[slot],
            device_id={AXES[axis]: hop(here[axis], k)},
            device_id_type=MESH,
        )

    def go(op):
        op.start()
        started.append(op)

    def coords(p):
        return tuple(here[axis] for axis in PARTS[p][0])

    def first(p, way, origin, source=None):
        a, b, t = coords(p)
        return copy(
            cell(PARTS[p], origin, b, t, (c,)), p * 3 + way, PARTS[p][0][0], NEAR[way], source
        )

    def second(p, way, k, line, half):
        t = coords(p)[2]
        at = cell(PARTS[p], two(half), line, t, (c,))
        return copy(at, 9 + (p * 2 + way) * 3 + k, PARTS[p][0][1], NEAR[way])

    def third(p, sub, way, k, t, half):
        line = hop(coords(p)[1], LINES[sub])
        at = cell(PARTS[p], two(half), line, t, (c,))
        return copy(at, 27 + ((p * 4 + sub) * 2 + way) * 3 + k, PARTS[p][0][2], NEAR[way])

    def pair_copy(p, k, at):
        return pltpu.make_async_remote_copy(
            src_ref=hid_ref.at[at], dst_ref=hid_ref.at[at],
            send_sem=sib_send.at[p * 13 + k], recv_sem=sib_recv.at[p * 13 + k],
            device_id=sibling, device_id_type=MESH,
        )

    def pair_plane(p, core):
        return pair_copy(p, 0, cell(PARTS[p], slice(None), slice(None), coords(p)[2], (core,)))

    def pair_line(p, sub, way, core):
        _, b, t = coords(p)
        at = cell(PARTS[p], slice(None), hop(b, LINES[sub]), hop(t, BACK[way]), (core,))
        return pair_copy(p, 1 + sub * 3 + way, at)

    def send_line(p, sub):
        for k in range(2):
            for way in range(2):
                go(third(p, sub, way, k, coords(p)[2], way if k == 0 else 1 - way))

    def pass_line(p, sub):
        for way in range(2):
            near = hop(coords(p)[2], BACK[way])
            third(p, sub, way, 0, near, way).wait_recv()
            go(third(p, sub, way, 2, near, way))

    def finish_line(p, sub):
        for way in range(2):
            third(p, sub, way, 1, hop(coords(p)[2], BACK[way]), 1 - way).wait_recv()
            go(pair_line(p, sub, way, c))
        for way in range(2):
            third(p, sub, way, 2, hop(coords(p)[2], 2), way).wait_recv()
        go(pair_line(p, sub, 2, c))

    parts = range(3)
    for way in (2, 0, 1):
        for p in parts:
            _, row, rows = PARTS[p]
            go(first(p, way, coords(p)[0], shard.at[pl.ds(row, rows), :]))
    own_hidden.wait()
    for p in parts:
        a, b, t = coords(p)
        for way in range(3):
            first(p, way, hop(a, BACK[way])).wait_recv()
        for k in range(2):
            for way in range(2):
                go(second(p, way, k, b, way if k == 0 else 1 - way))
        send_line(p, 0)
    for p in parts:
        b = coords(p)[1]
        for way in range(2):
            near = hop(b, BACK[way])
            second(p, way, 0, near, way).wait_recv()
            go(second(p, way, 2, near, way))
    for p in parts:
        pass_line(p, 0)
    for p in parts:
        b = coords(p)[1]
        for way in range(2):
            second(p, way, 1, hop(b, BACK[way]), 1 - way).wait_recv()
            send_line(p, 1 + way)
    for p in parts:
        for way in range(2):
            second(p, way, 2, hop(coords(p)[1], 2), way).wait_recv()
        send_line(p, 3)
        go(pair_plane(p, c))
    for sub in (1, 2):
        for p in parts:
            pass_line(p, sub)
    for p in parts:
        finish_line(p, 0)
    for p in parts:
        pass_line(p, 3)
    for sub in (1, 2, 3):
        for p in parts:
            finish_line(p, sub)
    for p in parts:
        pair_plane(p, 1 - c).wait_recv()
        for sub in range(4):
            for way in range(3):
                pair_line(p, sub, way, 1 - c).wait_recv()
    for op in started:
        op.wait_send()
    docs_pair(c).wait_send()
    for blk in range(4):
        op = pltpu.make_async_copy(
            hid_ref.at[
                y, z, x, blk // 2,
                pl.ds(pl.multiple_of(blk % 2 * DOCS + c * HALF, 16), HALF), slice(None),
            ],
            mask_ref.at[pl.ds(blk * HALF, HALF), :],
            own_sem.at[blk],
        )
        op.start()
    for blk in range(4):
        pltpu.make_async_copy(
            mask_ref.at[pl.ds(blk * HALF, HALF), :], mask_ref.at[pl.ds(blk * HALF, HALF), :], own_sem.at[blk]
        ).wait()

    def drain_docs(o, carry):
        docs_copy(same_core(o), me).wait_send()
        return carry

    def drain_weight(o, carry):
        weight_copy(lax.rem(me + o, 32), me).wait_send()
        return carry

    lax.fori_loop(1, 16, drain_docs, 0)
    lax.fori_loop(1, 32, drain_weight, 0)


def expand(keys, docs_t, expand_weight):
    vmem = pl.BlockSpec(memory_space=pltpu.VMEM)
    return pl.pallas_call(
        expand_kernel,
        out_shape=(
            jax.ShapeDtypeStruct((4, 4, 4, 2, SHARD, BLK), jnp.bfloat16),
            jax.ShapeDtypeStruct((16, 2, 32, 256), jnp.bfloat16),
            jax.ShapeDtypeStruct((SHARD, BLK), jnp.bfloat16),
            jax.ShapeDtypeStruct((8, LBLK_DEV * SLOTS), jnp.int32),
        ),
        in_specs=[vmem, vmem, pl.BlockSpec(memory_space=pltpu.HBM)],
        out_specs=(pl.BlockSpec(memory_space=pl.ANY), vmem, vmem, vmem),
        scratch_shapes=[
            pltpu.VMEM((32, 256), jnp.bfloat16),
            pltpu.VMEM((16, 2, 32, 256), jnp.bfloat16),
            pltpu.VMEM((SHARD, BLK), jnp.bfloat16),
            pltpu.SemaphoreType.DMA((32,)),
            pltpu.SemaphoreType.DMA((32,)),
            pltpu.SemaphoreType.DMA((32,)),
            pltpu.SemaphoreType.DMA((32,)),
            pltpu.SemaphoreType.DMA((5,)),
            pltpu.SemaphoreType.DMA((99,)),
            pltpu.SemaphoreType.DMA((99,)),
            pltpu.SemaphoreType.DMA((39,)),
            pltpu.SemaphoreType.DMA((39,)),
        ],
        compiler_params=pltpu.CompilerParams(
            collective_id=0, has_side_effects=True, vmem_limit_bytes=36 * MIB
        ),
        name="expand",
    )(keys, docs_t, expand_weight)


def label_kernel(
    tables, base, pos_ref, hid_ref, weight_ref, gs_ref, gp_ref,
    h, h_t, w, res, pos_b, gp, h_sem, w_sem, gp_sem,
):
    g = pl.program_id(0)

    def block_copy(p):
        b = lax.div(tables[0, p * NAMED], 512)
        return pltpu.make_async_copy(hid_ref.at[b], h.at[p], h_sem.at[p])

    def weight_copy(q):
        return pltpu.make_async_copy(weight_ref.at[q], w.at[q], w_sem.at[q])

    @pl.when(g == 0)
    def _():
        def begin(p, carry):
            block_copy(p).start()
            return carry

        lax.fori_loop(0, POOL, begin, 0)

        def begin_weight(q, carry):
            weight_copy(q).start()
            return carry

        lax.fori_loop(0, LBLK_DEV, begin_weight, 0)
        turned = pos_ref[...].T
        for k in range(POS):
            pos_b[k] = jnp.broadcast_to(turned[:, k : k + 1], (DOCS, BLK))

        def arrive(p, carry):
            block_copy(p).wait()
            h_t[p] = h[p].T
            return carry

        lax.fori_loop(0, POOL, arrive, 0, unroll=8)

    rows = [g * STEP + k for k in range(STEP)]
    spots = [[tables[1, q * SLOTS + s] for s in range(SLOTS)] for q in rows]
    for q in rows:
        weight_copy(q).wait()
    scores = []
    for q, where in zip(rows, spots):
        logits = jnp.zeros((DOCS, BLK), jnp.float32)
        for s in range(0, SLOTS, 2):
            left = jnp.concatenate([h[where[s]], h[where[s + 1]]], axis=1)
            right = w[q, s : s + 2].reshape(2 * BLK, BLK)
            logits += jnp.dot(left, right, preferred_element_type=jnp.float32)
        scores.append(logits)
    residuals = []
    for q, logits in zip(rows, scores):
        ids = (base[0] + q) * BLK + lax.broadcasted_iota(jnp.int32, (DOCS, BLK), 1)
        hit = pos_b[0] == ids
        for k in range(1, POS):
            hit = jnp.logical_or(hit, pos_b[k] == ids)
        residual = (jax.nn.sigmoid(logits) - jnp.where(hit, 1.0, 0.0)).astype(jnp.bfloat16)
        res[q] = residual
        residuals.append(residual)
    for k, (where, residual) in enumerate(zip(spots, residuals)):
        for s in range(SLOTS):
            gs_ref[k, s] = jnp.dot(
                h_t[where[s]], residual, preferred_element_type=jnp.float32
            ).astype(jnp.bfloat16)

    def gp_copy(f):
        return pltpu.make_async_copy(
            gp.at[pl.ds(f * 24, 24)], gp_ref.at[pl.ds(f * 24, 24)], gp_sem.at[f]
        )

    @pl.when(g == LBLK_DEV // STEP - 1)
    def _():
        for f in range(4):

            def collect(p, carry):
                slots = [lax.rem(tables[0, p * NAMED + k], 512) for k in range(NAMED)]
                pairs = [(lax.div(i, SLOTS), lax.rem(i, SLOTS)) for i in slots]
                left = jnp.concatenate([res[q] for q, _ in pairs], axis=1)
                right = jnp.concatenate([w[q, s] for q, s in pairs], axis=1)
                gp[p] = lax.dot_general(
                    left, right, (((1,), (1,)), ((), ())), preferred_element_type=jnp.float32
                ).astype(jnp.bfloat16)
                return carry

            lax.fori_loop(f * 24, f * 24 + 24, collect, 0, unroll=8)
            gp_copy(f).start()
        for f in range(4):
            gp_copy(f).wait()


def label_blocks(tables, base, positives, hid, sparse_weight):
    return pl.pallas_call(
        label_kernel,
        out_shape=(
            jax.ShapeDtypeStruct((LBLK_DEV, SLOTS, BLK, BLK), jnp.bfloat16),
            jax.ShapeDtypeStruct((POOL, DOCS, BLK), jnp.bfloat16),
        ),
        grid_spec=pltpu.PrefetchScalarGridSpec(
            num_scalar_prefetch=2,
            grid=(LBLK_DEV // STEP,),
            in_specs=[
                pl.BlockSpec((POS, DOCS), lambda g, *_: (0, 0)),
                pl.BlockSpec(memory_space=pl.ANY),
                pl.BlockSpec(memory_space=pl.ANY),
            ],
            out_specs=(
                pl.BlockSpec((STEP, SLOTS, BLK, BLK), lambda g, *_: (g, 0, 0, 0)),
                pl.BlockSpec(memory_space=pl.ANY),
            ),
            scratch_shapes=[
                pltpu.VMEM((POOL, DOCS, BLK), jnp.bfloat16),
                pltpu.VMEM((POOL, BLK, DOCS), jnp.bfloat16),
                pltpu.VMEM((LBLK_DEV, SLOTS, BLK, BLK), jnp.bfloat16),
                pltpu.VMEM((LBLK_DEV, DOCS, BLK), jnp.bfloat16),
                pltpu.VMEM((POS, DOCS, BLK), jnp.int32),
                pltpu.VMEM((POOL, DOCS, BLK), jnp.bfloat16),
                pltpu.SemaphoreType.DMA((POOL,)),
                pltpu.SemaphoreType.DMA((LBLK_DEV,)),
                pltpu.SemaphoreType.DMA((4,)),
            ],
        ),
        compiler_params=pltpu.CompilerParams(
            dimension_semantics=("arbitrary",), vmem_limit_bytes=36 * MIB
        ),
        name="label_blocks",
    )(tables, base, positives, hid, sparse_weight)


def reduce_kernel(
    tables, gp_ref, mask, docs_ref, out_ref,
    own, sib, acc, grad, mine_grad, pieces, *rest,
):
    across2, near2, across1, near1, near0 = (rest[k * 3 : k * 3 + 3] for k in range(5))
    pair_sem, send, recv, o_send, o_recv = rest[15:]
    y, z, x, c = (lax.axis_index(a) for a in AXES)
    here = (y, z, x)
    sibling = {"label_2": 1 - c}
    me = z * 8 + x * 2 + c
    barrier = pltpu.get_barrier_semaphore()

    def greet(o, carry):
        pl.semaphore_signal(
            barrier, inc=1, device_id=label_peer(lax.rem(me + o, 32)), device_id_type=MESH
        )
        return carry

    lax.fori_loop(1, 32, greet, 0)
    for k in (1, 2, 3):
        pl.semaphore_signal(barrier, inc=1, device_id={"feat": hop(y, k)}, device_id_type=MESH)

    def docs_half(k):
        return gp_ref.at[:, pl.ds(pl.multiple_of(k * HALF, 16), HALF), :]

    to_pair = pltpu.make_async_remote_copy(
        src_ref=docs_half(1 - c), dst_ref=sib.at[pl.ds(0, POOL)],
        send_sem=pair_sem.at[0], recv_sem=pair_sem.at[1],
        device_id=sibling, device_id_type=MESH,
    )
    mine = pltpu.make_async_copy(docs_half(c), own.at[pl.ds(0, POOL)], pair_sem.at[2])
    mine.start()
    own[POOL] = jnp.zeros((HALF, BLK), jnp.bfloat16)
    sib[POOL] = jnp.zeros((HALF, BLK), jnp.bfloat16)
    pl.semaphore_wait(barrier, 34)
    to_pair.start()
    mine.wait()
    to_pair.wait()

    parts = range(3)
    started = []

    def coords(p):
        return tuple(here[axis] for axis in PARTS[p][0])

    def spread(p, sub):
        order, row, rows = PARTS[p]
        line = hop(coords(p)[1], LINES[sub])

        def one(i, carry):
            at = cell(PARTS[p], lax.div(i, 4), line, lax.rem(i, 4))
            first_block = ((at[0] * 4 + at[1]) * 4 + at[2]) * 4
            for blk in range(row // HALF, (row + rows - 1) // HALF + 1):
                low, high = max(row, blk * HALF), min(row + rows, blk * HALF + HALF)
                span = pl.ds(low - blk * HALF, high - low)
                b = first_block + blk
                acc[(*at[:3], pl.ds(low, high - low), slice(None))] = (
                    own[tables[2, b], span, :] + sib[tables[3, b], span, :]
                )
            return carry

        lax.fori_loop(0, 16, one, 0)

    def push(source, target, slot, axis, k):
        return pltpu.make_async_remote_copy(
            src_ref=acc.at[source], dst_ref=target, send_sem=send.at[slot], recv_sem=recv.at[slot],
            device_id={AXES[axis]: hop(here[axis], k)}, device_id_type=MESH,
        )

    def go(op):
        op.start()
        started.append(op)

    def third(p, sub, way, k):
        line, t = hop(coords(p)[1], LINES[sub]), coords(p)[2]
        half = 1 - way if k == 1 else way
        source = cell(PARTS[p], two(half), line, hop(t, 2 if k == 0 else NEAR[way]))
        target = across2[p].at[sub, way] if k == 0 else near2[p].at[sub, way, two(half)]
        slot = 27 + ((p * 4 + sub) * 2 + way) * 3 + k
        return push(source, target, slot, PARTS[p][0][2], NEAR[way])

    def second(p, way, k):
        _, b, t = coords(p)
        half = 1 - way if k == 1 else way
        source = cell(PARTS[p], two(half), hop(b, 2 if k == 0 else NEAR[way]), t)
        target = across1[p].at[way] if k == 0 else near1[p].at[way, two(half)]
        return push(source, target, 9 + (p * 2 + way) * 3 + k, PARTS[p][0][1], NEAR[way])

    def first(p, way):
        a, b, t = coords(p)
        source = cell(PARTS[p], hop(a, NEAR[way]), b, t)
        return push(source, near0[p].at[way], p * 3 + way, PARTS[p][0][0], NEAR[way])

    def add(at, *terms):
        total = acc[at].astype(jnp.float32)
        for term in terms:
            total = total + term.astype(jnp.float32)
        acc[at] = total.astype(jnp.bfloat16)

    def send_line(p, sub):
        spread(p, sub)
        for k in range(2):
            for way in range(2):
                go(third(p, sub, way, k))

    def pass_line(p, sub):
        line, t = hop(coords(p)[1], LINES[sub]), coords(p)[2]
        for way in range(2):
            third(p, sub, way, 0).wait_recv()
            for i in range(2):
                add(
                    cell(PARTS[p], 2 * way + i, line, hop(t, NEAR[way])),
                    across2[p][sub, way, i],
                )
            go(third(p, sub, way, 2))

    def finish_line(p, sub):
        line, t = hop(coords(p)[1], LINES[sub]), coords(p)[2]
        for way in range(2):
            third(p, sub, way, 1).wait_recv()
            third(p, sub, way, 2).wait_recv()
        for i in range(4):
            add(cell(PARTS[p], i, line, t), near2[p][sub, 0, i], near2[p][sub, 1, i])

    for p in parts:
        send_line(p, 3)
    for p in parts:
        send_line(p, 1)
    for p in parts:
        pass_line(p, 3)
        send_line(p, 2)
    for p in parts:
        pass_line(p, 1)
        send_line(p, 0)
    for p in parts:
        finish_line(p, 3)
        for way in range(2):
            go(second(p, way, 0))
    for p in parts:
        pass_line(p, 2)
    for p in parts:
        pass_line(p, 0)
    for p in parts:
        finish_line(p, 1)
        finish_line(p, 2)
        for way in range(2):
            go(second(p, way, 1))
    for p in parts:
        _, b, t = coords(p)
        for way in range(2):
            second(p, way, 0).wait_recv()
            for i in range(2):
                add(cell(PARTS[p], 2 * way + i, hop(b, NEAR[way]), t), across1[p][way, i])
            go(second(p, way, 2))
    for p in parts:
        finish_line(p, 0)
    for p in parts:
        _, b, t = coords(p)
        for way in range(2):
            second(p, way, 1).wait_recv()
            second(p, way, 2).wait_recv()
        for i in range(4):
            add(cell(PARTS[p], i, b, t), near1[p][0, i], near1[p][1, i])
        for way in (2, 0, 1):
            go(first(p, way))
    for p in parts:
        for way in range(3):
            first(p, way).wait_recv()
        add(cell(PARTS[p], *coords(p)), *(near0[p][way] for way in range(3)))

    total = acc[y, z, x]
    grad[...] = jnp.where(mask[...] > 0, total, jnp.zeros_like(total))

    def columns(k):
        return grad.at[pl.ds(pl.multiple_of(k * DOCS, 16), DOCS), :]

    def pair_grad(k, core):
        return pltpu.make_async_remote_copy(
            src_ref=columns(k), dst_ref=mine_grad.at[core],
            send_sem=pair_sem.at[3], recv_sem=pair_sem.at[4],
            device_id=sibling, device_id_type=MESH,
        )

    to_other = pair_grad(1 - c, c)
    to_other.start()
    kept = pltpu.make_async_copy(columns(c), mine_grad.at[c], pair_sem.at[5])
    kept.start()
    kept.wait()
    pair_grad(c, 1 - c).wait_recv()
    sides = [
        jnp.concatenate([mine_grad[half, pl.ds(j * HALF, HALF), :] for half in range(2)], axis=0)
        for j in range(2)
    ]
    right = jnp.concatenate(sides, axis=1)

    def out_columns(l):
        return out_ref.at[:, pl.ds(pl.multiple_of(l * 256, 256), 256)]

    def out_copy(to, origin):
        return pltpu.make_async_remote_copy(
            src_ref=pieces.at[to], dst_ref=out_columns(origin),
            send_sem=o_send.at[to], recv_sem=o_recv.at[origin],
            device_id=label_peer(to), device_id_type=MESH,
        )

    own_out = pltpu.make_async_copy(pieces.at[me], out_columns(me), pair_sem.at[6])
    for k in range(4):
        row = hop(z, k) * 8
        left = docs_ref[pl.ds(hop(z, k) * 4, 4)].reshape(256, 256)[:, :DOCS]
        pieces[pl.ds(row, 8)] = jnp.dot(
            left, right, preferred_element_type=jnp.float32
        ).astype(jnp.bfloat16).reshape(8, 32, 256)

        def deliver(o, carry):
            out_copy(row + lax.rem(x * 2 + c + o, 8), me).start()
            return carry

        lax.fori_loop(1 if k == 0 else 0, 8, deliver, 0)
        if k == 0:
            own_out.start()
    own_out.wait()

    def collect(o, carry):
        other = lax.rem(me + o, 32)
        out_copy(other, other).wait_recv()
        return carry

    def drain(o, carry):
        out_copy(lax.rem(me + o, 32), me).wait_send()
        return carry

    lax.fori_loop(1, 32, collect, 0)
    to_other.wait_send()
    for op in started:
        op.wait_send()
    lax.fori_loop(1, 32, drain, 0)


def reduce_blocks(tables, gp, mask, docs_all):
    received = [
        pltpu.VMEM((*lead, rows, BLK), jnp.bfloat16)
        for lead in ((4, 2, 2), (4, 2, 4), (2, 2), (2, 4), (3,))
        for _, _, rows in PARTS
    ]
    return pl.pallas_call(
        reduce_kernel,
        out_shape=jax.ShapeDtypeStruct((32, 8192), jnp.bfloat16),
        in_specs=[
            pl.BlockSpec(memory_space=pltpu.SMEM),
            pl.BlockSpec(memory_space=pl.ANY),
            pl.BlockSpec(memory_space=pltpu.VMEM),
            pl.BlockSpec(memory_space=pltpu.VMEM),
        ],
        out_specs=pl.BlockSpec(memory_space=pltpu.VMEM),
        scratch_shapes=[
            pltpu.VMEM((POOL + 1, HALF, BLK), jnp.bfloat16),
            pltpu.VMEM((POOL + 1, HALF, BLK), jnp.bfloat16),
            pltpu.VMEM((4, 4, 4, SHARD, BLK), jnp.bfloat16),
            pltpu.VMEM((SHARD, BLK), jnp.bfloat16),
            pltpu.VMEM((2, DOCS, BLK), jnp.bfloat16),
            pltpu.VMEM((32, 32, 256), jnp.bfloat16),
            *received,
            pltpu.SemaphoreType.DMA((7,)),
            pltpu.SemaphoreType.DMA((99,)),
            pltpu.SemaphoreType.DMA((99,)),
            pltpu.SemaphoreType.DMA((32,)),
            pltpu.SemaphoreType.DMA((32,)),
        ],
        compiler_params=pltpu.CompilerParams(
            collective_id=1, has_side_effects=True, vmem_limit_bytes=24 * MIB
        ),
        name="reduce_blocks",
    )(tables, gp, mask, docs_all)


def on_device(documents, expand_weight, sparse_weight, feature_lists, positives):
    core = lax.axis_index("label_2")
    group = lax.axis_index(AXES)
    pair = lax.dynamic_slice_in_dim(feature_lists, (group - core) * LBLK_DEV, 2 * LBLK_DEV, 0)
    pair = pair.reshape(2, LBLK_DEV * SLOTS)
    keys = jnp.where(core == 0, pair, pair[::-1]) * 512
    keys = jnp.pad(keys + jnp.arange(LBLK_DEV * SLOTS, dtype=jnp.int32)[None, :], ((0, 6), (0, 0)))
    hid, docs_all, mask, tables = expand(keys, documents.T, expand_weight)
    grad_sparse, gp = label_blocks(
        tables,
        (group * LBLK_DEV).astype(jnp.int32).reshape(1),
        positives.T,
        hid.reshape(FBLOCKS, DOCS, BLK),
        sparse_weight,
    )
    grad_expand = reduce_blocks(tables, gp, mask, docs_all)
    return (grad_expand, grad_sparse)


def solution(mesh):
    finer = Mesh(mesh.devices.reshape(mesh.shape["feat"], 4, 4, 2), AXES)
    return jax.shard_map(
        on_device,
        mesh=finer,
        in_specs=(P(None, LABEL), P(LABEL, "feat"), P(AXES, None, None, None), P(), P()),
        out_specs=(P(LABEL, "feat"), P(AXES, None, None, None)),
        check_vma=False,
    )
```

time: 180 us -> 145 us (0.81)
  between operations: 14.2 us -> 0.72 us
  Pallas kernels: 150 us -> 139 us
  local copies, waits for them, and re-layouts: 14.2 us -> 4.5 us
    unnamed x12 -> x9, local copies, waits for them, and re-layouts: 11.6 us -> 4.15 us
    pallas_call x1, Pallas kernels: 55.1 us -> 47.9 us  [reduce_blocks(): pl.pallas_call(reduce_kernel, out_shape=jax.ShapeDtypeStruct((32, 8192),...]
    pallas_call x1, Pallas kernels: 57.7 us -> 53.4 us  [expand(): pl.pallas_call(expand_kernel, out_shape=(jax.ShapeDtypeStruct((4, 4, 4, 2...]
where the time goes in v3:
time: 145 us
  Pallas kernels  139 us (96%)
  local copies, waits for them, and re-layouts  4.5 us (3%)
    pallas_call x1, Pallas kernels, expand(): pl.pallas_call(expand_kernel, out_shape=(jax.ShapeDtypeStruct((4, 4, 4, 2...  53.4 us
    pallas_call x1, Pallas kernels, reduce_blocks(): pl.pallas_call(reduce_kernel, out_shape=jax.ShapeDtypeStruct((32, 8192),...  47.9 us
    pallas_call x1, Pallas kernels, label_blocks(): pl.pallas_call(label_kernel, out_shape=(jax.ShapeDtypeStruct((LBLK_DEV, S...  38.1 us
    unnamed x9, local copies, waits for them, and re-layouts  4.15 us

profile of v3, /device:TPU:1, one launch (start us, length us, event | category | flops | bytes accessed | tf_op | source)
XLA Modules:
  0.0 144.7 jit_solution(5101307411759374942)
XLA Ops:
  0.6 0.0 copy-start
  0.7 0.9 copy-done
  1.6 0.1 constant_dynamic-slice_fusion
  1.6 0.1 copy.8
  1.7 0.1 reshape.13
  1.8 0.1 rev.3
  2.0 0.0 copy-start.1
  2.0 1.0 copy-done.1
  3.0 0.0 copy-start.2
  3.0 0.7 copy-done.2
  3.7 53.4 %expand.1 = (bf16[4,4,4,2,320,128]{5,4,3,2,1,0:T(8,128)(2,1)S(1)}, bf16[16,2,32,256]{3,2,1,0:T(8,128)(2,1)S(1)}, bf16[320,128]{1,0:T(8,128)(2,1)S(1)}, s32[8,384]{1,0:T(8,128)S(1)}) custom-call(s32[8,384]{1,0:T(8,128)S(1)} %pad.4.keys_ref, bf16[32,160]{1,0:T(8,128)(2,1)S(1)} %bitcast.5, bf16[32,8192]{1,0:T(8,128)(2,1)S(1)} %copy-done.1), custom_call_target="tpu_custom_call" | custom-call | tf_op jit(solution)/shard_map/expand/pallas_call | solution.py:320
  57.1 0.0 copy-start.3
  57.1 0.7 copy-done.3
  57.8 38.1 %label_blocks.1 = (bf16[24,16,128,128]{3,2,1,0:T(8,128)(2,1)}, bf16[96,160,128]{2,1,0:T(8,128)(2,1)S(1)}) custom-call(s32[8,384]{1,0:T(8,128)S(1)} %get-tuple-element.8.tables, s32[1]{0:T(128)} %bitcast.1.base, s32[8,160]{1,0:T(8,128)S(1)} %bitcast.6, bf16[256,160,128]{2,1,0:T(8,128)(2,1)S(1)} %bitcast.4, bf16[24,16,128,128]{3,2,1,0:T(8,128)(2,1)} %weight_ref.3), custom_call_target="tpu_custom_call" | custom-call | tf_op jit(solution)/shard_map/label_blocks/pallas_call | solution.py:441
  96.0 47.9 %reduce_blocks.1 = bf16[32,8192]{1,0:T(8,128)(2,1)S(1)} custom-call(s32[8,384]{1,0:T(8,128)S(1)} %get-tuple-element.8.tables, bf16[96,160,128]{2,1,0:T(8,128)(2,1)S(1)} %get-tuple-element.10.gp_ref, bf16[320,128]{1,0:T(8,128)(2,1)S(1)} %get-tuple-element.11.mask, bf16[16,2,32,256]{3,2,1,0:T(8,128)(2,1)S(1)} %get-tuple-element.12.docs_ref), custom_call_target="tpu_custom_call" | custom-call | tf_op jit(solution)/shard_map/reduce_blocks/pallas_call | solution.py:722
  143.9 0.8 copy.10
  (2 shorter events, 0.0 us)
Async XLA Ops:
  0.6 0.9 copy-start
  2.0 1.0 copy-start.1
  3.0 0.7 copy-start.2
  57.1 0.7 copy-start.3

commit v4 on v3

--- a/solution.py
+++ b/solution.py
@@ -14,6 +14,8 @@
 LBLK_DEV = 24
 POOL = 96
 STEP = 4
+STEPS = 6
+SPAN = 16
 NAMED = 4
 POS = 8
 DOCS = 160
@@ -67,6 +69,7 @@
             tables_ref[0:1, :] = jnp.sum(sort, axis=0, keepdims=True).astype(jnp.int32)
             above = jnp.sum(jnp.where(col < row, 1.0, 0.0), axis=0, keepdims=True)
             tables_ref[1:2, :] = lax.shift_right_logical(above.astype(jnp.int32), 2)
+            tables_ref[4:5, :] = lax.shift_right_logical(row, 9)
         place = lax.shift_right_logical(below, 2)
         first = jnp.where(place * NAMED == below, place - POOL, 0).astype(jnp.float32)
         hit = lax.shift_right_logical(col, 9) == lanes[:, :FBLOCKS]
@@ -349,92 +352,75 @@
 
 
 def label_kernel(
-    tables, base, pos_ref, hid_ref, weight_ref, gs_ref, gp_ref,
-    h, h_t, w, res, pos_b, gp, h_sem, w_sem, gp_sem,
+    tables, base, pos_ref, hid, weight_ref, gs_ref, gp_ref, h_t, w, res, pos_b, gp, w_sem, gp_sem,
 ):
-    g = pl.program_id(0)
-
-    def block_copy(p):
-        b = lax.div(tables[0, p * NAMED], 512)
-        return pltpu.make_async_copy(hid_ref.at[b], h.at[p], h_sem.at[p])
-
-    def weight_copy(q):
-        return pltpu.make_async_copy(weight_ref.at[q], w.at[q], w_sem.at[q])
-
-    @pl.when(g == 0)
+    step = pl.program_id(0)
+
+    def weight_copy(k):
+        part = pl.ds(k * STEP, STEP)
+        return pltpu.make_async_copy(weight_ref.at[part], w.at[part], w_sem.at[k])
+
+    def gp_copy(k):
+        part = pl.ds(k * SPAN, SPAN)
+        return pltpu.make_async_copy(gp.at[part], gp_ref.at[part], gp_sem.at[k])
+
+    @pl.when(step == 0)
     def _():
-        def begin(p, carry):
-            block_copy(p).start()
-            return carry
-
-        lax.fori_loop(0, POOL, begin, 0)
-
-        def begin_weight(q, carry):
-            weight_copy(q).start()
-            return carry
-
-        lax.fori_loop(0, LBLK_DEV, begin_weight, 0)
+        for k in range(STEPS):
+            weight_copy(k).start()
         turned = pos_ref[...].T
         for k in range(POS):
             pos_b[k] = jnp.broadcast_to(turned[:, k : k + 1], (DOCS, BLK))
 
-        def arrive(p, carry):
-            block_copy(p).wait()
-            h_t[p] = h[p].T
-            return carry
-
-        lax.fori_loop(0, POOL, arrive, 0, unroll=8)
-
-    rows = [g * STEP + k for k in range(STEP)]
-    spots = [[tables[1, q * SLOTS + s] for s in range(SLOTS)] for q in rows]
-    for q in rows:
-        weight_copy(q).wait()
-    scores = []
-    for q, where in zip(rows, spots):
-        logits = jnp.zeros((DOCS, BLK), jnp.float32)
-        for s in range(0, SLOTS, 2):
-            left = jnp.concatenate([h[where[s]], h[where[s + 1]]], axis=1)
-            right = w[q, s : s + 2].reshape(2 * BLK, BLK)
-            logits += jnp.dot(left, right, preferred_element_type=jnp.float32)
-        scores.append(logits)
-    residuals = []
-    for q, logits in zip(rows, scores):
-        ids = (base[0] + q) * BLK + lax.broadcasted_iota(jnp.int32, (DOCS, BLK), 1)
-        hit = pos_b[0] == ids
-        for k in range(1, POS):
-            hit = jnp.logical_or(hit, pos_b[k] == ids)
-        residual = (jax.nn.sigmoid(logits) - jnp.where(hit, 1.0, 0.0)).astype(jnp.bfloat16)
-        res[q] = residual
-        residuals.append(residual)
-    for k, (where, residual) in enumerate(zip(spots, residuals)):
-        for s in range(SLOTS):
-            gs_ref[k, s] = jnp.dot(
-                h_t[where[s]], residual, preferred_element_type=jnp.float32
+    def listed(place):
+        return hid[lax.div(tables[0, place * NAMED], 512)]
+
+    @pl.when(step < STEPS)
+    def _():
+        weight_copy(step).wait()
+        for k in range(STEP):
+            q = step * STEP + k
+            logits = jnp.zeros((DOCS, BLK), jnp.float32)
+            for s in range(0, SLOTS, 2):
+                left = jnp.concatenate(
+                    [hid[tables[4, q * SLOTS + s + i]] for i in range(2)], axis=1
+                )
+                right = w[q, s : s + 2].reshape(2 * BLK, BLK)
+                logits += jnp.dot(left, right, preferred_element_type=jnp.float32)
+            ids = (base[0] + q) * BLK + lax.broadcasted_iota(jnp.int32, (DOCS, BLK), 1)
+            hit = pos_b[0] == ids
+            for i in range(1, POS):
+                hit = jnp.logical_or(hit, pos_b[i] == ids)
+            res[q] = (jax.nn.sigmoid(logits) - jnp.where(hit, 1.0, 0.0)).astype(jnp.bfloat16)
+        for k in range(SPAN):
+            place = step * SPAN + k
+            h_t[place] = listed(place).T
+
+    @pl.when(step >= STEPS)
+    def _():
+        late = step - STEPS
+        for k in range(STEP):
+            q = late * STEP + k
+            residual = res[q]
+            for s in range(SLOTS):
+                gs_ref[k, s] = jnp.dot(
+                    h_t[tables[1, q * SLOTS + s]], residual, preferred_element_type=jnp.float32
+                ).astype(jnp.bfloat16)
+        for k in range(SPAN):
+            place = late * SPAN + k
+            slots = [lax.rem(tables[0, place * NAMED + i], 512) for i in range(NAMED)]
+            pairs = [(lax.div(i, SLOTS), lax.rem(i, SLOTS)) for i in slots]
+            left = jnp.concatenate([res[q] for q, _ in pairs], axis=1)
+            right = jnp.concatenate([w[q, s] for q, s in pairs], axis=1)
+            gp[place] = lax.dot_general(
+                left, right, (((1,), (1,)), ((), ())), preferred_element_type=jnp.float32
             ).astype(jnp.bfloat16)
-
-    def gp_copy(f):
-        return pltpu.make_async_copy(
-            gp.at[pl.ds(f * 24, 24)], gp_ref.at[pl.ds(f * 24, 24)], gp_sem.at[f]
-        )
-
-    @pl.when(g == LBLK_DEV // STEP - 1)
+        gp_copy(late).start()
+
+    @pl.when(step == 2 * STEPS - 1)
     def _():
-        for f in range(4):
-
-            def collect(p, carry):
-                slots = [lax.rem(tables[0, p * NAMED + k], 512) for k in range(NAMED)]
-                pairs = [(lax.div(i, SLOTS), lax.rem(i, SLOTS)) for i in slots]
-                left = jnp.concatenate([res[q] for q, _ in pairs], axis=1)
-                right = jnp.concatenate([w[q, s] for q, s in pairs], axis=1)
-                gp[p] = lax.dot_general(
-                    left, right, (((1,), (1,)), ((), ())), preferred_element_type=jnp.float32
-                ).astype(jnp.bfloat16)
-                return carry
-
-            lax.fori_loop(f * 24, f * 24 + 24, collect, 0, unroll=8)
-            gp_copy(f).start()
-        for f in range(4):
-            gp_copy(f).wait()
+        for k in range(STEPS):
+            gp_copy(k).wait()
 
 
 def label_blocks(tables, base, positives, hid, sparse_weight):
@@ -446,26 +432,26 @@
         ),
         grid_spec=pltpu.PrefetchScalarGridSpec(
             num_scalar_prefetch=2,
-            grid=(LBLK_DEV // STEP,),
+            grid=(2 * STEPS,),
             in_specs=[
                 pl.BlockSpec((POS, DOCS), lambda g, *_: (0, 0)),
-                pl.BlockSpec(memory_space=pl.ANY),
+                pl.BlockSpec(memory_space=pltpu.VMEM),
                 pl.BlockSpec(memory_space=pl.ANY),
             ],
             out_specs=(
-                pl.BlockSpec((STEP, SLOTS, BLK, BLK), lambda g, *_: (g, 0, 0, 0)),
+                pl.BlockSpec(
+                    (STEP, SLOTS, BLK, BLK), lambda g, *_: (jnp.maximum(g - STEPS, 0), 0, 0, 0)
+                ),
                 pl.BlockSpec(memory_space=pl.ANY),
             ),
             scratch_shapes=[
-                pltpu.VMEM((POOL, DOCS, BLK), jnp.bfloat16),
                 pltpu.VMEM((POOL, BLK, DOCS), jnp.bfloat16),
                 pltpu.VMEM((LBLK_DEV, SLOTS, BLK, BLK), jnp.bfloat16),
                 pltpu.VMEM((LBLK_DEV, DOCS, BLK), jnp.bfloat16),
                 pltpu.VMEM((POS, DOCS, BLK), jnp.int32),
                 pltpu.VMEM((POOL, DOCS, BLK), jnp.bfloat16),
-                pltpu.SemaphoreType.DMA((POOL,)),
-                pltpu.SemaphoreType.DMA((LBLK_DEV,)),
-                pltpu.SemaphoreType.DMA((4,)),
+                pltpu.SemaphoreType.DMA((STEPS,)),
+                pltpu.SemaphoreType.DMA((STEPS,)),
             ],
         ),
         compiler_params=pltpu.CompilerParams(

time: 145 us -> 130 us (0.90)
  Pallas kernels: 139 us -> 125 us
    pallas_call x1, Pallas kernels: 38.1 us -> 23.6 us  [label_blocks(): pl.pallas_call(label_kernel, out_shape=(jax.ShapeDtypeStruct((LBLK_DEV, S...]
where the time goes in v4:
time: 130 us
  Pallas kernels  125 us (96%)
  local copies, waits for them, and re-layouts  4.5 us (3%)
    pallas_call x1, Pallas kernels, expand(): pl.pallas_call(expand_kernel, out_shape=(jax.ShapeDtypeStruct((4, 4, 4, 2...  53.4 us
    pallas_call x1, Pallas kernels, reduce_blocks(): pl.pallas_call(reduce_kernel, out_shape=jax.ShapeDtypeStruct((32, 8192),...  47.8 us
    pallas_call x1, Pallas kernels, label_blocks(): pl.pallas_call(label_kernel, out_shape=(jax.ShapeDtypeStruct((LBLK_DEV, S...  23.6 us
    unnamed x9, local copies, waits for them, and re-layouts  4.15 us

profile of v4, /device:TPU:1, one launch (start us, length us, event | category | flops | bytes accessed | tf_op | source)
XLA Modules:
  0.0 130.0 jit_solution(13649837199147947391)
XLA Ops:
  0.6 0.0 copy-start
  0.7 0.9 copy-done
  1.6 0.1 constant_dynamic-slice_fusion
  1.6 0.1 copy.8
  1.7 0.1 reshape.13
  1.8 0.1 rev.3
  2.0 0.0 copy-start.1
  2.0 1.0 copy-done.1
  3.0 0.0 copy-start.2
  3.0 0.7 copy-done.2
  3.7 53.4 %expand.1 = (bf16[4,4,4,2,320,128]{5,4,3,2,1,0:T(8,128)(2,1)S(1)}, bf16[16,2,32,256]{3,2,1,0:T(8,128)(2,1)S(1)}, bf16[320,128]{1,0:T(8,128)(2,1)S(1)}, s32[8,384]{1,0:T(8,128)S(1)}) custom-call(s32[8,384]{1,0:T(8,128)S(1)} %pad.4.keys_ref, bf16[32,160]{1,0:T(8,128)(2,1)S(1)} %bitcast.5, bf16[32,8192]{1,0:T(8,128)(2,1)S(1)} %copy-done.1), custom_call_target="tpu_custom_call" | custom-call | tf_op jit(solution)/shard_map/expand/pallas_call | solution.py:323
  57.1 0.0 copy-start.3
  57.1 0.7 copy-done.3
  57.8 23.6 %label_blocks.1 = (bf16[24,16,128,128]{3,2,1,0:T(8,128)(2,1)}, bf16[96,160,128]{2,1,0:T(8,128)(2,1)S(1)}) custom-call(s32[8,384]{1,0:T(8,128)S(1)} %get-tuple-element.8.tables, s32[1]{0:T(128)} %bitcast.1.base, s32[8,160]{1,0:T(8,128)S(1)} %bitcast.6, bf16[256,160,128]{2,1,0:T(8,128)(2,1)S(1)} %bitcast.4, bf16[24,16,128,128]{3,2,1,0:T(8,128)(2,1)} %weight_ref.3), custom_call_target="tpu_custom_call" | custom-call | tf_op jit(solution)/shard_map/label_blocks/pallas_call | solution.py:427
  81.4 47.8 %reduce_blocks.1 = bf16[32,8192]{1,0:T(8,128)(2,1)S(1)} custom-call(s32[8,384]{1,0:T(8,128)S(1)} %get-tuple-element.8.tables, bf16[96,160,128]{2,1,0:T(8,128)(2,1)S(1)} %get-tuple-element.10.gp_ref, bf16[320,128]{1,0:T(8,128)(2,1)S(1)} %get-tuple-element.11.mask, bf16[16,2,32,256]{3,2,1,0:T(8,128)(2,1)S(1)} %get-tuple-element.12.docs_ref), custom_call_target="tpu_custom_call" | custom-call | tf_op jit(solution)/shard_map/reduce_blocks/pallas_call | solution.py:708
  129.2 0.8 copy.10
  (2 shorter events, 0.0 us)
Async XLA Ops:
  0.6 0.9 copy-start
  2.0 1.0 copy-start.1
  3.0 0.7 copy-start.2
  57.1 0.7 copy-start.3

commit v5 on v4

--- a/solution.py
+++ b/solution.py
@@ -285,12 +285,6 @@
             finish_line(p, sub)
     for p in parts:
         pair_plane(p, 1 - c).wait_recv()
-        for sub in range(4):
-            for way in range(3):
-                pair_line(p, sub, way, 1 - c).wait_recv()
-    for op in started:
-        op.wait_send()
-    docs_pair(c).wait_send()
     for blk in range(4):
         op = pltpu.make_async_copy(
             hid_ref.at[
@@ -298,14 +292,20 @@
                 pl.ds(pl.multiple_of(blk % 2 * DOCS + c * HALF, 16), HALF), slice(None),
             ],
             mask_ref.at[pl.ds(blk * HALF, HALF), :],
-            own_sem.at[blk],
+            own_sem.at[5 + blk],
         )
         op.start()
+    for p in parts:
+        for sub in range(4):
+            for way in range(3):
+                pair_line(p, sub, way, 1 - c).wait_recv()
+    for op in started:
+        op.wait_send()
     for blk in range(4):
         pltpu.make_async_copy(
-            mask_ref.at[pl.ds(blk * HALF, HALF), :], mask_ref.at[pl.ds(blk * HALF, HALF), :], own_sem.at[blk]
+            mask_ref.at[pl.ds(blk * HALF, HALF), :], mask_ref.at[pl.ds(blk * HALF, HALF), :], own_sem.at[5 + blk]
         ).wait()
-
+    docs_pair(c).wait_send()
     def drain_docs(o, carry):
         docs_copy(same_core(o), me).wait_send()
         return carry
@@ -338,7 +338,7 @@
             pltpu.SemaphoreType.DMA((32,)),
             pltpu.SemaphoreType.DMA((32,)),
             pltpu.SemaphoreType.DMA((32,)),
-            pltpu.SemaphoreType.DMA((5,)),
+            pltpu.SemaphoreType.DMA((9,)),
             pltpu.SemaphoreType.DMA((99,)),
             pltpu.SemaphoreType.DMA((99,)),
             pltpu.SemaphoreType.DMA((39,)),
@@ -473,15 +473,10 @@
     me = z * 8 + x * 2 + c
     barrier = pltpu.get_barrier_semaphore()
 
-    def greet(o, carry):
-        pl.semaphore_signal(
-            barrier, inc=1, device_id=label_peer(lax.rem(me + o, 32)), device_id_type=MESH
-        )
-        return carry
-
-    lax.fori_loop(1, 32, greet, 0)
-    for k in (1, 2, 3):
-        pl.semaphore_signal(barrier, inc=1, device_id={"feat": hop(y, k)}, device_id_type=MESH)
+    for axis, m in zip(AXES, here):
+        for k in (1, 3):
+            pl.semaphore_signal(barrier, inc=1, device_id={axis: hop(m, k)}, device_id_type=MESH)
+    pl.semaphore_signal(barrier, inc=1, device_id=sibling, device_id_type=MESH)
 
     def docs_half(k):
         return gp_ref.at[:, pl.ds(pl.multiple_of(k * HALF, 16), HALF), :]
@@ -495,7 +490,7 @@
     mine.start()
     own[POOL] = jnp.zeros((HALF, BLK), jnp.bfloat16)
     sib[POOL] = jnp.zeros((HALF, BLK), jnp.bfloat16)
-    pl.semaphore_wait(barrier, 34)
+    pl.semaphore_wait(barrier, 7)
     to_pair.start()
     mine.wait()
     to_pair.wait()
@@ -743,7 +738,8 @@
     pair = pair.reshape(2, LBLK_DEV * SLOTS)
     keys = jnp.where(core == 0, pair, pair[::-1]) * 512
     keys = jnp.pad(keys + jnp.arange(LBLK_DEV * SLOTS, dtype=jnp.int32)[None, :], ((0, 6), (0, 0)))
-    hid, docs_all, mask, tables = expand(keys, documents.T, expand_weight)
+    weight = pltpu.with_memory_space_constraint(expand_weight, pltpu.HBM)
+    hid, docs_all, mask, tables = expand(keys, documents.T, weight)
     grad_sparse, gp = label_blocks(
         tables,
         (group * LBLK_DEV).astype(jnp.int32).reshape(1),

time: 130 us -> 128 us (0.985)
  Pallas kernels: 125 us -> 123 us
    pallas_call x1, Pallas kernels: 47.8 us -> 46.4 us  [reduce_blocks(): pl.pallas_call(reduce_kernel, out_shape=jax.ShapeDtypeStruct((32, 8192),...]
    unnamed x9 -> x7, local copies, waits for them, and re-layouts: 4.15 us -> 3.11 us
where the time goes in v5:
time: 128 us; the launch traced here: 127 us
  Pallas kernels  123 us (96%)
  local copies, waits for them, and re-layouts  3.46 us (3%)
    pallas_call x1, Pallas kernels, expand(): pl.pallas_call(expand_kernel, out_shape=(jax.ShapeDtypeStruct((4, 4, 4, 2...  53.3 us
    pallas_call x1, Pallas kernels, reduce_blocks(): pl.pallas_call(reduce_kernel, out_shape=jax.ShapeDtypeStruct((32, 8192),...  46.4 us
    pallas_call x1, Pallas kernels, label_blocks(): pl.pallas_call(label_kernel, out_shape=(jax.ShapeDtypeStruct((LBLK_DEV, S...  23.6 us
    unnamed x7, local copies, waits for them, and re-layouts  3.11 us

profile of v5, /device:TPU:1, one launch (start us, length us, event | category | flops | bytes accessed | tf_op | source)
XLA Modules:
  0.0 127.4 jit_solution(9107328454590665428)
XLA Ops:
  0.6 0.0 copy-start
  0.7 0.9 copy-done
  1.6 0.1 constant_dynamic-slice_fusion
  1.6 0.1 copy.8
  1.7 0.1 reshape.13
  1.8 0.1 rev.3
  2.0 0.0 copy-start.1
  2.0 0.7 copy-done.1
  2.7 53.3 %expand.1 = (bf16[4,4,4,2,320,128]{5,4,3,2,1,0:T(8,128)(2,1)S(1)}, bf16[16,2,32,256]{3,2,1,0:T(8,128)(2,1)S(1)}, bf16[320,128]{1,0:T(8,128)(2,1)S(1)}, s32[8,384]{1,0:T(8,128)S(1)}) custom-call(s32[8,384]{1,0:T(8,128)S(1)} %pad.4.keys_ref, bf16[32,160]{1,0:T(8,128)(2,1)S(1)} %bitcast.5, bf16[32,8192]{1,0:T(8,128)(2,1)} %weight_ref.2), custom_call_target="tpu_custom_call" | custom-call | tf_op jit(solution)/shard_map/expand/pallas_call | solution.py:323
  56.0 0.0 copy-start.2
  56.0 0.7 copy-done.2
  56.7 23.6 %label_blocks.1 = (bf16[24,16,128,128]{3,2,1,0:T(8,128)(2,1)}, bf16[96,160,128]{2,1,0:T(8,128)(2,1)S(1)}) custom-call(s32[8,384]{1,0:T(8,128)S(1)} %get-tuple-element.8.tables, s32[1]{0:T(128)} %bitcast.1.base, s32[8,160]{1,0:T(8,128)S(1)} %bitcast.6, bf16[256,160,128]{2,1,0:T(8,128)(2,1)S(1)} %bitcast.4, bf16[24,16,128,128]{3,2,1,0:T(8,128)(2,1)} %weight_ref.3), custom_call_target="tpu_custom_call" | custom-call | tf_op jit(solution)/shard_map/label_blocks/pallas_call | solution.py:427
  80.2 46.4 %reduce_blocks.1 = bf16[32,8192]{1,0:T(8,128)(2,1)S(1)} custom-call(s32[8,384]{1,0:T(8,128)S(1)} %get-tuple-element.8.tables, bf16[96,160,128]{2,1,0:T(8,128)(2,1)S(1)} %get-tuple-element.10.gp_ref, bf16[320,128]{1,0:T(8,128)(2,1)S(1)} %get-tuple-element.11.mask, bf16[16,2,32,256]{3,2,1,0:T(8,128)(2,1)S(1)} %get-tuple-element.12.docs_ref), custom_call_target="tpu_custom_call" | custom-call | tf_op jit(solution)/shard_map/reduce_blocks/pallas_call | solution.py:703
  126.6 0.8 copy.10
  (2 shorter events, 0.0 us)
Async XLA Ops:
  0.6 0.9 copy-start
  2.0 0.7 copy-start.1
  56.0 0.7 copy-start.2

commit v6 on v5

--- a/solution.py
+++ b/solution.py
@@ -78,7 +78,7 @@
 
 
 def expand_kernel(
-    keys_ref, docs_in, weight_ref, hid_ref, docs_all, mask_ref, tables_ref, docs_ref, w_all, shard,
+    keys_ref, docs_in, weight_ref, hid_ref, docs_all, mask_ref, tables_ref, docs_small, docs_ref, w_all, shard,
     w_send, w_recv, d_send, d_recv, own_sem, send, recv, sib_send, sib_recv,
 ):
     y, z, x, c = (lax.axis_index(a) for a in AXES)
@@ -86,8 +86,8 @@
     me = z * 8 + x * 2 + c
     sibling = {"label_2": 1 - c}
     peer = label_peer
-    docs_ref[:, 0:DOCS] = docs_in[...]
-    docs_ref[:, DOCS:] = jnp.zeros((32, 256 - DOCS), jnp.bfloat16)
+    load = pltpu.make_async_copy(docs_in, docs_small, own_sem.at[9])
+    load.start()
     barrier = pltpu.get_barrier_semaphore()
 
     def greet(o, carry):
@@ -99,6 +99,9 @@
     lax.fori_loop(1, 32, greet, 0)
     for k in (1, 2, 3):
         pl.semaphore_signal(barrier, inc=1, device_id={"feat": hop(y, k)}, device_id_type=MESH)
+    load.wait()
+    docs_ref[:, 0:DOCS] = docs_small[...]
+    docs_ref[:, DOCS:] = jnp.zeros((32, 256 - DOCS), jnp.bfloat16)
     pl.semaphore_wait(barrier, 34)
 
     def rows_of(ref, l):
@@ -328,9 +331,10 @@
             jax.ShapeDtypeStruct((SHARD, BLK), jnp.bfloat16),
             jax.ShapeDtypeStruct((8, LBLK_DEV * SLOTS), jnp.int32),
         ),
-        in_specs=[vmem, vmem, pl.BlockSpec(memory_space=pltpu.HBM)],
+        in_specs=[vmem, pl.BlockSpec(memory_space=pl.ANY), pl.BlockSpec(memory_space=pl.ANY)],
         out_specs=(pl.BlockSpec(memory_space=pl.ANY), vmem, vmem, vmem),
         scratch_shapes=[
+            pltpu.VMEM((32, DOCS), jnp.bfloat16),
             pltpu.VMEM((32, 256), jnp.bfloat16),
             pltpu.VMEM((16, 2, 32, 256), jnp.bfloat16),
             pltpu.VMEM((SHARD, BLK), jnp.bfloat16),
@@ -338,7 +342,7 @@
             pltpu.SemaphoreType.DMA((32,)),
             pltpu.SemaphoreType.DMA((32,)),
             pltpu.SemaphoreType.DMA((32,)),
-            pltpu.SemaphoreType.DMA((9,)),
+            pltpu.SemaphoreType.DMA((10,)),
             pltpu.SemaphoreType.DMA((99,)),
             pltpu.SemaphoreType.DMA((99,)),
             pltpu.SemaphoreType.DMA((39,)),
@@ -352,7 +356,8 @@
 
 
 def label_kernel(
-    tables, base, pos_ref, hid, weight_ref, gs_ref, gp_ref, h_t, w, res, pos_b, gp, w_sem, gp_sem,
+    tables, base, pos_ref, hid, weight_ref, gs_ref, gp_ref,
+    pos, h_t, w, res, pos_b, gp, w_sem, gp_sem, pos_sem,
 ):
     step = pl.program_id(0)
 
@@ -366,9 +371,12 @@
 
     @pl.when(step == 0)
     def _():
+        load = pltpu.make_async_copy(pos_ref, pos, pos_sem)
+        load.start()
         for k in range(STEPS):
             weight_copy(k).start()
-        turned = pos_ref[...].T
+        load.wait()
+        turned = pos[...].T
         for k in range(POS):
             pos_b[k] = jnp.broadcast_to(turned[:, k : k + 1], (DOCS, BLK))
 
@@ -434,7 +442,7 @@
             num_scalar_prefetch=2,
             grid=(2 * STEPS,),
             in_specs=[
-                pl.BlockSpec((POS, DOCS), lambda g, *_: (0, 0)),
+                pl.BlockSpec(memory_space=pl.ANY),
                 pl.BlockSpec(memory_space=pltpu.VMEM),
                 pl.BlockSpec(memory_space=pl.ANY),
             ],
@@ -445,6 +453,7 @@
                 pl.BlockSpec(memory_space=pl.ANY),
             ),
             scratch_shapes=[
+                pltpu.VMEM((POS, DOCS), jnp.int32),
                 pltpu.VMEM((POOL, BLK, DOCS), jnp.bfloat16),
                 pltpu.VMEM((LBLK_DEV, SLOTS, BLK, BLK), jnp.bfloat16),
                 pltpu.VMEM((LBLK_DEV, DOCS, BLK), jnp.bfloat16),
@@ -452,6 +461,7 @@
                 pltpu.VMEM((POOL, DOCS, BLK), jnp.bfloat16),
                 pltpu.SemaphoreType.DMA((STEPS,)),
                 pltpu.SemaphoreType.DMA((STEPS,)),
+                pltpu.SemaphoreType.DMA,
             ],
         ),
         compiler_params=pltpu.CompilerParams(
@@ -739,11 +749,12 @@
     keys = jnp.where(core == 0, pair, pair[::-1]) * 512
     keys = jnp.pad(keys + jnp.arange(LBLK_DEV * SLOTS, dtype=jnp.int32)[None, :], ((0, 6), (0, 0)))
     weight = pltpu.with_memory_space_constraint(expand_weight, pltpu.HBM)
-    hid, docs_all, mask, tables = expand(keys, documents.T, weight)
+    docs_t = pltpu.with_memory_space_constraint(documents.T, pltpu.HBM)
+    hid, docs_all, mask, tables = expand(keys, docs_t, weight)
     grad_sparse, gp = label_blocks(
         tables,
         (group * LBLK_DEV).astype(jnp.int32).reshape(1),
-        positives.T,
+        pltpu.with_memory_space_constraint(positives.T, pltpu.HBM),
         hid.reshape(FBLOCKS, DOCS, BLK),
         sparse_weight,
     )

time: 128 us -> 130 us (1.016)
  Pallas kernels: 123 us -> 127 us
  local copies, waits for them, and re-layouts: 3.46 us -> 2.06 us
    pallas_call x1, Pallas kernels: 23.6 us -> 26.8 us  [label_blocks(): pl.pallas_call(label_kernel, out_shape=(jax.ShapeDtypeStruct((LBLK_DEV, S...]
    unnamed x7 -> x3, local copies, waits for them, and re-layouts: 3.11 us -> 1.7 us
where the time goes in v6:
time: 130 us; the launch traced here: 129 us
  Pallas kernels  127 us (98%)
  local copies, waits for them, and re-layouts  2.06 us (2%)
    pallas_call x1, Pallas kernels, expand(): pl.pallas_call(expand_kernel, out_shape=(jax.ShapeDtypeStruct((4, 4, 4, 2...  53.4 us
    pallas_call x1, Pallas kernels, reduce_blocks(): pl.pallas_call(reduce_kernel, out_shape=jax.ShapeDtypeStruct((32, 8192),...  46.4 us
    pallas_call x1, Pallas kernels, label_blocks(): pl.pallas_call(label_kernel, out_shape=(jax.ShapeDtypeStruct((LBLK_DEV, S...  26.8 us

profile of v6, /device:TPU:1, one launch (start us, length us, event | category | flops | bytes accessed | tf_op | source)
XLA Modules:
  0.0 129.4 jit_solution(2832831986827341472)
XLA Ops:
  0.6 0.0 copy-start
  0.7 0.9 copy-done
  1.6 0.1 constant_dynamic-slice_fusion
  1.6 0.1 copy.8
  1.7 0.1 reshape.13
  1.8 0.1 rev.3
  2.0 53.4 %expand.1 = (bf16[4,4,4,2,320,128]{5,4,3,2,1,0:T(8,128)(2,1)S(1)}, bf16[16,2,32,256]{3,2,1,0:T(8,128)(2,1)S(1)}, bf16[320,128]{1,0:T(8,128)(2,1)S(1)}, s32[8,384]{1,0:T(8,128)S(1)}) custom-call(s32[8,384]{1,0:T(8,128)S(1)} %pad.4.keys_ref, bf16[32,160]{1,0:T(8,128)(2,1)} %bitcast.5, bf16[32,8192]{1,0:T(8,128)(2,1)} %weight_ref.2), custom_call_target="tpu_custom_call" | custom-call | tf_op jit(solution)/shard_map/expand/pallas_call | solution.py:326
  55.4 26.8 %label_blocks.1 = (bf16[24,16,128,128]{3,2,1,0:T(8,128)(2,1)}, bf16[96,160,128]{2,1,0:T(8,128)(2,1)S(1)}) custom-call(s32[8,384]{1,0:T(8,128)S(1)} %get-tuple-element.8.tables, s32[1]{0:T(128)} %bitcast.1.base, s32[8,160]{1,0:T(8,128)} %bitcast.6, bf16[256,160,128]{2,1,0:T(8,128)(2,1)S(1)} %bitcast.4, bf16[24,16,128,128]{3,2,1,0:T(8,128)(2,1)} %weight_ref.3), custom_call_target="tpu_custom_call" | custom-call | tf_op jit(solution)/shard_map/label_blocks/pallas_call | solution.py:435
  82.2 46.4 %reduce_blocks.1 = bf16[32,8192]{1,0:T(8,128)(2,1)S(1)} custom-call(s32[8,384]{1,0:T(8,128)S(1)} %get-tuple-element.8.tables, bf16[96,160,128]{2,1,0:T(8,128)(2,1)S(1)} %get-tuple-element.10.gp_ref, bf16[320,128]{1,0:T(8,128)(2,1)S(1)} %get-tuple-element.11.mask, bf16[16,2,32,256]{3,2,1,0:T(8,128)(2,1)S(1)} %get-tuple-element.12.docs_ref), custom_call_target="tpu_custom_call" | custom-call | tf_op jit(solution)/shard_map/reduce_blocks/pallas_call | solution.py:713
  128.6 0.8 copy.10
  (2 shorter events, 0.0 us)
Async XLA Ops:
  0.6 0.9 copy-start

commit v7 on v6

--- a/solution.py
+++ b/solution.py
@@ -356,8 +356,7 @@
 
 
 def label_kernel(
-    tables, base, pos_ref, hid, weight_ref, gs_ref, gp_ref,
-    pos, h_t, w, res, pos_b, gp, w_sem, gp_sem, pos_sem,
+    tables, base, pos_ref, hid, weight_ref, gs_ref, gp_ref, h_t, w, res, pos_b, gp, w_sem, gp_sem,
 ):
     step = pl.program_id(0)
 
@@ -371,12 +370,9 @@
 
     @pl.when(step == 0)
     def _():
-        load = pltpu.make_async_copy(pos_ref, pos, pos_sem)
-        load.start()
         for k in range(STEPS):
             weight_copy(k).start()
-        load.wait()
-        turned = pos[...].T
+        turned = pos_ref[...].T
         for k in range(POS):
             pos_b[k] = jnp.broadcast_to(turned[:, k : k + 1], (DOCS, BLK))
 
@@ -442,7 +438,7 @@
             num_scalar_prefetch=2,
             grid=(2 * STEPS,),
             in_specs=[
-                pl.BlockSpec(memory_space=pl.ANY),
+                pl.BlockSpec((POS, DOCS), lambda g, *_: (0, 0)),
                 pl.BlockSpec(memory_space=pltpu.VMEM),
                 pl.BlockSpec(memory_space=pl.ANY),
             ],
@@ -453,7 +449,6 @@
                 pl.BlockSpec(memory_space=pl.ANY),
             ),
             scratch_shapes=[
-                pltpu.VMEM((POS, DOCS), jnp.int32),
                 pltpu.VMEM((POOL, BLK, DOCS), jnp.bfloat16),
                 pltpu.VMEM((LBLK_DEV, SLOTS, BLK, BLK), jnp.bfloat16),
                 pltpu.VMEM((LBLK_DEV, DOCS, BLK), jnp.bfloat16),
@@ -461,7 +456,6 @@
                 pltpu.VMEM((POOL, DOCS, BLK), jnp.bfloat16),
                 pltpu.SemaphoreType.DMA((STEPS,)),
                 pltpu.SemaphoreType.DMA((STEPS,)),
-                pltpu.SemaphoreType.DMA,
             ],
         ),
         compiler_params=pltpu.CompilerParams(
@@ -503,7 +497,7 @@
     pl.semaphore_wait(barrier, 7)
     to_pair.start()
     mine.wait()
-    to_pair.wait()
+    to_pair.wait_recv()
 
     parts = range(3)
     started = []
@@ -698,6 +692,7 @@
         return carry
 
     lax.fori_loop(1, 32, collect, 0)
+    to_pair.wait_send()
     to_other.wait_send()
     for op in started:
         op.wait_send()
@@ -754,7 +749,7 @@
     grad_sparse, gp = label_blocks(
         tables,
         (group * LBLK_DEV).astype(jnp.int32).reshape(1),
-        pltpu.with_memory_space_constraint(positives.T, pltpu.HBM),
+        positives.T,
         hid.reshape(FBLOCKS, DOCS, BLK),
         sparse_weight,
     )

time: 130 us -> 127 us (0.977)
  Pallas kernels: 127 us -> 123 us
    pallas_call x1, Pallas kernels: 26.8 us -> 23.6 us  [label_blocks(): pl.pallas_call(label_kernel, out_shape=(jax.ShapeDtypeStruct((LBLK_DEV, S...]
where the time goes in v7:
time: 127 us
  Pallas kernels  123 us (97%)
  local copies, waits for them, and re-layouts  2.75 us (2%)
    pallas_call x1, Pallas kernels, expand(): pl.pallas_call(expand_kernel, out_shape=(jax.ShapeDtypeStruct((4, 4, 4, 2...  53.4 us
    pallas_call x1, Pallas kernels, reduce_blocks(): pl.pallas_call(reduce_kernel, out_shape=jax.ShapeDtypeStruct((32, 8192),...  46.4 us
    pallas_call x1, Pallas kernels, label_blocks(): pl.pallas_call(label_kernel, out_shape=(jax.ShapeDtypeStruct((LBLK_DEV, S...  23.6 us

profile of v7, /device:TPU:1, one launch (start us, length us, event | category | flops | bytes accessed | tf_op | source)
XLA Modules:
  0.0 126.8 jit_solution(2060804004356098464)
XLA Ops:
  0.6 0.0 copy-start
  0.7 0.9 copy-done
  1.6 0.1 constant_dynamic-slice_fusion
  1.6 0.1 copy.8
  1.7 0.1 reshape.13
  1.8 0.1 rev.3
  2.0 53.4 %expand.1 = (bf16[4,4,4,2,320,128]{5,4,3,2,1,0:T(8,128)(2,1)S(1)}, bf16[16,2,32,256]{3,2,1,0:T(8,128)(2,1)S(1)}, bf16[320,128]{1,0:T(8,128)(2,1)S(1)}, s32[8,384]{1,0:T(8,128)S(1)}) custom-call(s32[8,384]{1,0:T(8,128)S(1)} %pad.4.keys_ref, bf16[32,160]{1,0:T(8,128)(2,1)} %bitcast.6, bf16[32,8192]{1,0:T(8,128)(2,1)} %weight_ref.2), custom_call_target="tpu_custom_call" | custom-call | tf_op jit(solution)/shard_map/expand/pallas_call | solution.py:326
  55.4 0.0 copy-start.1
  55.4 0.7 copy-done.1
  56.1 23.6 %label_blocks.1 = (bf16[24,16,128,128]{3,2,1,0:T(8,128)(2,1)}, bf16[96,160,128]{2,1,0:T(8,128)(2,1)S(1)}) custom-call(s32[8,384]{1,0:T(8,128)S(1)} %get-tuple-element.8.tables, s32[1]{0:T(128)} %bitcast.1.base, s32[8,160]{1,0:T(8,128)S(1)} %bitcast.5, bf16[256,160,128]{2,1,0:T(8,128)(2,1)S(1)} %bitcast.4, bf16[24,16,128,128]{3,2,1,0:T(8,128)(2,1)} %weight_ref.3), custom_call_target="tpu_custom_call" | custom-call | tf_op jit(solution)/shard_map/label_blocks/pallas_call | solution.py:431
  79.7 46.4 %reduce_blocks.1 = bf16[32,8192]{1,0:T(8,128)(2,1)S(1)} custom-call(s32[8,384]{1,0:T(8,128)S(1)} %get-tuple-element.8.tables, bf16[96,160,128]{2,1,0:T(8,128)(2,1)S(1)} %get-tuple-element.10.gp_ref, bf16[320,128]{1,0:T(8,128)(2,1)S(1)} %get-tuple-element.11.mask, bf16[16,2,32,256]{3,2,1,0:T(8,128)(2,1)S(1)} %get-tuple-element.12.docs_ref), custom_call_target="tpu_custom_call" | custom-call | tf_op jit(solution)/shard_map/reduce_blocks/pallas_call | solution.py:708
  126.0 0.8 copy.10
  (2 shorter events, 0.0 us)
Async XLA Ops:
  0.6 0.9 copy-start
  55.4 0.7 copy-start.1
